TPU v7x, 32 devices: a whole 2x2x4 slice. The times are simulated.
32 devices in a mesh: mem: 2 (over x), gy: 4 (over z), gx: 4 (over y, core).
Axes of the slice: x: 2, y: 2, z: 4, core: 2. Of those that a mesh axis runs over, the one named last changes fastest.
Arguments:
- alpha: float32 [16, 32, 64, 512], P('mem', None, 'gy', 'gx'), may hold values from -4 to 4
- perturb: bfloat16 [16, 4, 32, 64, 512], P('mem', None, None, 'gy', 'gx'), may hold values from -6 to 6
- chi: float32 [4, 32, 64, 512], P(None, None, 'gy', 'gx'), may hold values from -4 to 4
- kappa: float32 [64, 512], P('gy', 'gx'), may hold values from 0.05 to 0.24
- vert_bounds: int32 [2, 32], replicated, may hold values from 0 to 31, as said below
- static_vert: float32 [4, 32, 32], replicated, may hold values from -1 to 1
- fine_owner: int32 [16, 2], P(('gy', 'gx')), may hold values from 0 to 1, each once within a row
- obs_stencil: int32 [32768], P(('mem', 'gy', 'gx')), may hold values from 0 to 959
- obs_weight: float32 [4, 32768], P(None, ('mem', 'gy', 'gx')), may hold values from 0.05 to 0.5
- background: bfloat16 [32768, 128], P(('mem', 'gy', 'gx')), may hold values from -6 to 6
- observed: float32 [8, 32768], P(None, ('mem', 'gy', 'gx')), may hold values from -6 to 6
- inv_var: float32 [8, 32768], P(None, ('mem', 'gy', 'gx')), may hold values from 2 to 32
- jacobian: float32 [8, 128], replicated, may hold values from -0.5 to 0.5
- obs_count: int32 [32], P(('mem', 'gy', 'gx')), may hold values from 256 to 1024, as said below
Outputs:
- grad_alpha: float32 [16, 32, 64, 512], P('mem', None, 'gy', 'gx')
- grad_chi: float32 [4, 32, 64, 512], P(None, None, 'gy', 'gx')
Inputs may be any that keep to these rules, and one draw needn't show every extreme that they name: `vert_bounds`: row 0 holds each level's lowest and row 1 its highest coupled level; level l lies between both inclusive, and each lies 1 to 4 levels from l unless cut at the ends of the column. `obs_count`: observations below this count in a device's block are live; some device has exactly 1024 and some exactly 256.
All inputs are finite; a program needn't handle non-finite values.
Results may differ from a plain program's by a relative error of at most 0.00099.
Values may be sent and summed in bfloat16 or wider, within the bound.
A program may use at most 128 MiB of HBM per device.

v0:
```python
import math

import jax
import jax.numpy as jnp
from jax import lax
from jax.sharding import PartitionSpec as P

NDIFF = 4


ensemble_weight = 0.8
static_weight = 0.6
vertical_scale = 2.0
highest = lax.Precision.HIGHEST


def padded_2(cells, sides, width):
    for axis, dim in sides:
        count = lax.axis_size(axis)
        head = lax.slice_in_dim(cells, 0, width, axis=dim)
        tail = lax.slice_in_dim(cells, cells.shape[dim] - width, cells.shape[dim], axis=dim)
        cells = jnp.concatenate(
            [
                lax.ppermute(tail, axis, [(i, (i + 1) % count) for i in range(count)]),
                cells,
                lax.ppermute(head, axis, [((i + 1) % count, i) for i in range(count)]),
            ],
            axis=dim,
        )
    return cells


def shifted(value, axis, steps):
    count = lax.axis_size(axis)
    pairs = [(source, (source + steps) % count) for source in range(count)]
    return lax.ppermute(value, axis, pairs)


def vertical_matrix(vert_bounds, levels):
    row_level = lax.broadcasted_iota(jnp.int32, (levels, levels), 0)
    col_level = lax.broadcasted_iota(jnp.int32, (levels, levels), 1)
    inside = (col_level >= vert_bounds[0][:, None]) & (col_level <= vert_bounds[1][:, None])
    distance = jnp.abs(row_level - col_level).astype(jnp.float32)
    return jnp.where(inside, jnp.exp(-distance / vertical_scale), jnp.zeros_like(distance))


def deep_pad(values, margin):
    padded = padded_2(values, (("gy", 2), ("gx", 3)), margin)
    row_place = lax.axis_index("gy")
    upper_rows = jnp.flip(padded[:, :, margin : 2 * margin], axis=2)
    lower_rows = jnp.flip(padded[:, :, -2 * margin : -margin], axis=2)
    north_fixed = jnp.concatenate([upper_rows, padded[:, :, margin:]], axis=2)
    padded = jnp.where(row_place == 0, north_fixed, padded)
    south_fixed = jnp.concatenate([padded[:, :, :-margin], lower_rows], axis=2)
    return jnp.where(row_place == lax.axis_size("gy") - 1, south_fixed, padded)


def stencil_of(padded):
    center = padded[:, :, 1:-1, 1:-1]
    return (
        padded[:, :, :-2, 1:-1]
        + padded[:, :, 2:, 1:-1]
        + padded[:, :, 1:-1, :-2]
        + padded[:, :, 1:-1, 2:]
        - 4.0 * center
    )


def sweep_forward(padded, kappa_pad):
    for repeat in range(NDIFF):
        stencil_sum = stencil_of(padded)
        kappa_pad = kappa_pad[:, :, 1:-1, 1:-1]
        padded = padded[:, :, 1:-1, 1:-1] + kappa_pad * stencil_sum
    return padded


def sweep_adjoint(padded, kappa_pad):
    for repeat in range(NDIFF):
        stencil_sum = stencil_of(kappa_pad * padded)
        kappa_pad = kappa_pad[:, :, 1:-1, 1:-1]
        padded = padded[:, :, 1:-1, 1:-1] + stencil_sum
    return padded


def to_cells(values, column_width):
    return jnp.transpose(values.reshape(column_width, values.shape[2], values.shape[3]), (1, 2, 0))


def from_cells(cell_table, variables, levels):
    return jnp.transpose(cell_table, (2, 0, 1)).reshape(
        variables, levels, cell_table.shape[0], cell_table.shape[1]
    )


def extend_east(cell_table, rim_cols):
    rim_part = shifted(cell_table[:, :rim_cols], "gx", -1)
    return jnp.concatenate([cell_table, rim_part], axis=1)


def fold_east(wide_grad, tile_cols, rim_cols):
    from_west = shifted(wide_grad[:, tile_cols:], "gx", 1)
    head_cols = wide_grad[:, :rim_cols] + from_west
    return jnp.concatenate([head_cols, wide_grad[:, rim_cols:tile_cols]], axis=1)


def observe(region, obs_stencil, obs_weight, background, observed, inv_var, jacobian, obs_count):
    row_count, region_cols, column_width = region.shape
    band_size = region_cols - 1
    slot_table = region.reshape(row_count * region_cols, column_width)
    anchor_row = obs_stencil // band_size
    anchor_col = obs_stencil % band_size
    cell_index = [
        (anchor_row + corner // 2) * region_cols + anchor_col + corner % 2 for corner in range(4)
    ]
    increment_obs = jnp.zeros(background.shape, jnp.float32)
    for corner in range(4):
        picked = jnp.take(slot_table, cell_index[corner], axis=0).astype(jnp.float32)
        increment_obs = increment_obs + obs_weight[corner][:, None] * picked
    bent = jnp.tanh(background.astype(jnp.float32) + increment_obs)
    modeled = jnp.einsum("cv,ov->co", jacobian, bent, precision=highest)
    position = lax.broadcasted_iota(jnp.int32, modeled.shape, 1)
    misfit = jnp.where(
        position < obs_count[0], (modeled - observed) * inv_var, jnp.zeros_like(modeled)
    )
    state_grad = (1.0 - bent * bent) * jnp.einsum("co,cv->ov", misfit, jacobian, precision=highest)
    returned = jnp.zeros(slot_table.shape, jnp.float32)
    for corner in range(4):
        returned = returned.at[cell_index[corner]].add(obs_weight[corner][:, None] * state_grad)
    return returned.reshape(row_count, region_cols, column_width)


def body(
    alpha,
    perturb,
    chi,
    kappa,
    vert_bounds,
    static_vert,
    fine_owner,
    obs_stencil,
    obs_weight,
    background,
    observed,
    inv_var,
    jacobian,
    obs_count,
):
    members, levels, tile_rows, tile_cols = alpha.shape
    variables = perturb.shape[1]
    column_width = variables * levels
    member_groups = lax.axis_size("mem")
    band_width = tile_cols // member_groups
    shift_cols = band_width // 2
    rim_cols = shift_cols + 1
    member_group = lax.axis_index("mem")
    owner_row = fine_owner[0]
    band_ids = lax.broadcasted_iota(jnp.int32, (member_groups, member_groups), 1)
    own_band = jnp.sum(
        jnp.where(owner_row == member_group, band_ids[0], jnp.zeros_like(band_ids[0]))
    )
    region_offsets = lax.broadcasted_iota(jnp.int32, (band_width + 1,), 0)
    ens_scale = ensemble_weight / math.sqrt(members * member_groups - 1)
    vertical = vertical_matrix(vert_bounds, levels)
    spread = jnp.einsum("lm,kmyx->klyx", vertical, alpha, precision=highest)
    kappa_pad = deep_pad(kappa[None, None], NDIFF)
    spread = sweep_forward(deep_pad(spread, NDIFF), kappa_pad)
    partial_sum = jnp.sum(perturb.astype(jnp.float32) * spread[:, None], axis=0)
    member_total = lax.psum(partial_sum, "mem")
    static = jnp.einsum("vlm,vmyx->vlyx", static_vert, chi, precision=highest)
    increment = (ens_scale * member_total + static_weight * static).astype(jnp.bfloat16)
    widened = extend_east(to_cells(increment, column_width), rim_cols)
    own_cols = own_band * band_width + shift_cols + region_offsets
    region = jnp.take(widened, own_cols, axis=1)
    region_grad = observe(
        region, obs_stencil, obs_weight, background, observed, inv_var, jacobian, obs_count
    )
    wide_grad = jnp.zeros(widened.shape, jnp.float32).at[:, own_cols].add(region_grad)
    tile_grad = fold_east(wide_grad, tile_cols, rim_cols)
    gradient_cells = lax.psum(tile_grad, "mem")
    gradient = from_cells(gradient_cells, variables, levels)
    grad_chi = chi + static_weight * jnp.einsum(
        "vlm,vlyx->vmyx", static_vert, gradient, precision=highest
    )
    back_spread = ens_scale * jnp.sum(perturb.astype(jnp.float32) * gradient[None], axis=1)
    back_spread = sweep_adjoint(deep_pad(back_spread, NDIFF), kappa_pad)
    grad_alpha = alpha + jnp.einsum("lm,klyx->kmyx", vertical, back_spread, precision=highest)
    return (grad_alpha, grad_chi)


def solution(mesh):
    in_specs = (
        P("mem", None, "gy", "gx"),
        P("mem", None, None, "gy", "gx"),
        P(None, None, "gy", "gx"),
        P("gy", "gx"),
        P(),
        P(),
        P(("gy", "gx"), None),
        P(("mem", "gy", "gx")),
        P(None, ("mem", "gy", "gx")),
        P(("mem", "gy", "gx"), None),
        P(None, ("mem", "gy", "gx")),
        P(None, ("mem", "gy", "gx")),
        P(),
        P(("mem", "gy", "gx")),
    )
    out_specs = (P("mem", None, "gy", "gx"), P(None, None, "gy", "gx"))
    return jax.shard_map(body, mesh=mesh, in_specs=in_specs, out_specs=out_specs, check_vma=False)
```

profile of v0, /device:TPU:0, one launch (start us, length us, event | category | flops | bytes accessed | tf_op | source)
XLA Modules:
  0.0 409.0 jit_solution(9989891320124790640)
XLA Ops:
  13.8 3.9 fusion.28
  18.7 3.8 collective-permute-start.1
  27.2 8.3 %collective-permute-done = f32[8,32,4,128]{3,1,2,0:T(8,128)S(1)} collective-permute-done((f32[8,32,4,128]{3,1,2,0:T(8,128)}, f32[8,32,4,128]{3,1,2,0:T(8,128)S(1)}, u32[]{:S(2)}, u32[]{:S(2)}) %collective-permute-start) | collective-permute-done | bytes 524320 | tf_op jit(solution)/shard_map/ppermute | solution.py:24
  35.5 8.0 %collective-permute-done.1 = f32[8,32,4,128]{3,1,2,0:T(8,128)S(1)} collective-permute-done((f32[8,32,4,128]{3,1,2,0:T(8,128)}, f32[8,32,4,128]{3,1,2,0:T(8,128)S(1)}, u32[]{:S(2)}, u32[]{:S(2)}) %collective-permute-start.1) | collective-permute-done | bytes 524320 | tf_op jit(solution)/shard_map/ppermute | solution.py:26
  43.9 3.7 fusion.88
  55.1 11.1 %collective-permute-done.2 = f32[8,32,24,4]{1,2,3,0:T(8,128)} collective-permute-done((f32[8,32,24,4]{1,2,3,0:T(8,128)}, f32[8,32,24,4]{1,2,3,0:T(8,128)}, u32[]{:S(2)}, u32[]{:S(2)}) %collective-permute-start.2) | collective-permute-done | bytes 98336 | tf_op jit(solution)/shard_map/ppermute | solution.py:24
  72.9 5.7 %pad_maximum_fusion = f32[8,32,24,136]{3,1,2,0:T(8,128)S(1)} fusion(f32[8,32,24,4]{3,1,2,0:T(8,128)} %copy.55, f32[8,32,4,128]{3,1,2,0:T(8,128)S(1)} %collective-permute-done.1, f32[8,32,16,128]{3,1,2,0:T(8,128)S(1)} %fusion.28, f32[8,32,4,128]{3,1,2,0:T(8,128)S(1)} %collective-permute-done, f32[8,32,24,4]{3,1,2,0:T(8,128)} %copy.54), kind=kLoop, calls=%fused_computation.14 | loop fusion | flops 3342336 | bytes 6684672 | tf_op jit(solution)/shard_map/concatenate | solution.py:22
  87.5 6.6 %maximum_select_fusion = f32[8,32,24,136]{3,1,2,0:T(8,128)S(1)} fusion(f32[8,32,20,136]{3,1,2,0:T(8,128)} %slice.361, f32[8,32,4,136]{3,1,2,0:T(8,128)} %rev.20, pred[]{:T(512)S(6)} %eq.20, f32[8,32,24,4]{3,1,2,0:T(8,128)} %copy.55, f32[8,32,4,128]{3,1,2,0:T(8,128)S(1)} %collective-permute-done.1, f32[8,32,16,128]{3,1,2,0:T(8,128)S(1)} %fusion.28, ...), kind=kLoop, calls=%fused_computation.15 | loop fusion | flops 5013504 | bytes 10027009 | tf_op jit(solution)/shard_map/jit(_where)/select_n | solution.py:53
  99.6 5.9 %maximum_select_fusion.1 = f32[8,32,24,136]{3,1,2,0:T(8,128)S(1)} fusion(f32[8,32,24,136]{3,1,2,0:T(8,128)} %copy-done.2, f32[8,32,4,136]{3,1,2,0:T(8,128)S(1)} %copy-done.7, f32[8,32,20,136]{3,1,2,0:T(8,128)} %slice.362, pred[]{:T(512)S(6)} %eq.19), kind=kLoop, calls=%fused_computation.16 | loop fusion | flops 1671168 | bytes 10027009 | tf_op jit(solution)/shard_map/jit(_where)/select_n | solution.py:55
  105.5 6.1 %fusion.6 = f32[8,32,22,134]{3,1,2,0:T(8,128)S(1)} fusion(f32[8,32,24,136]{3,1,2,0:T(8,128)S(1)} %maximum_select_fusion.1, f32[22,134]{1,0:T(8,128)S(1)} %slice_bitcast_fusion.2), kind=kLoop, calls=%fused_computation.29 | loop fusion | flops 5282816 | bytes 18124304 | tf_op jit(solution)/shard_map/add | solution.py:73
  111.6 5.8 %fusion.11 = f32[8,32,20,132]{3,1,2,0:T(8,128)S(1)} fusion(f32[8,32,22,134]{3,1,2,0:T(8,128)S(1)} %fusion.6, f32[20,132]{1,0:T(8,128)S(1)} %slice_bitcast_fusion.1), kind=kLoop, calls=%fused_computation.41 | loop fusion | flops 4730880 | bytes 16230720 | tf_op jit(solution)/shard_map/add | solution.py:73
  117.4 5.0 %fusion.16 = f32[8,32,18,130]{3,1,2,0:T(8,128)S(1)} fusion(f32[8,32,20,132]{3,1,2,0:T(8,128)S(1)} %fusion.11, f32[18,130]{1,0:T(8,128)S(1)} %slice_bitcast_fusion), kind=kLoop, calls=%fused_computation.53 | loop fusion | flops 4193280 | bytes 14386320 | tf_op jit(solution)/shard_map/add | solution.py:73
  129.8 38.5 %all-reduce.3.cloned.1.call-done = f32[4,32,16,128]{3,1,2,0:T(8,128)} async-done(((f32[4,32,16,128]{3,1,2,0:T(8,128)}), f32[4,32,16,128]{3,1,2,0:T(8,128)}) %all-reduce.3.cloned.1.call-update) | async-done | bytes 1048592 | tf_op jit(solution)/shard_map/psum | solution.py:168
  192.6 6.7 %scatter_custom_fusion = f32[1040,128]{1,0:T(8,128)S(1)} fusion(s32[1024]{0:T(1024)S(1)} %get-tuple-element.64, f32[1024,128]{1,0:T(8,128)S(1)} %convolution_multiply_fusion.2, f32[]{:T(128)} %constant.45.clone.1, f32[1024]{0:T(1024)S(1)} %bitcast.96), kind=kCustom, calls=%fused_computation.103 | custom fusion | flops 262144 | bytes 1060868 | tf_op jit(solution)/shard_map/scatter-add | solution.py:128
  199.2 6.7 %scatter_custom_fusion.1 = f32[1040,128]{1,0:T(8,128)S(1)} fusion(f32[1040,128]{1,0:T(8,128)S(1)} %scatter_custom_fusion, s32[1024]{0:T(1024)S(1)} %get-tuple-element.59, f32[1024,128]{1,0:T(8,128)S(1)} %convolution_multiply_fusion.2, f32[1024]{0:T(1024)S(1)} %bitcast.94), kind=kCustom, calls=%fused_computation.101 | custom fusion | flops 262144 | bytes 1060864 | tf_op jit(solution)/shard_map/scatter-add | solution.py:128
  206.0 6.7 %scatter_custom_fusion.2 = f32[1040,128]{1,0:T(8,128)S(1)} fusion(f32[1040,128]{1,0:T(8,128)S(1)} %scatter_custom_fusion.1, s32[1024]{0:T(1024)S(1)} %get-tuple-element.49, f32[1024,128]{1,0:T(8,128)S(1)} %convolution_multiply_fusion.2, f32[1024]{0:T(1024)S(1)} %bitcast.92), kind=kCustom, calls=%fused_computation.99 | custom fusion | flops 262144 | bytes 1060864 | tf_op jit(solution)/shard_map/scatter-add | solution.py:128
  212.7 6.9 %scatter_custom_fusion.3 = f32[1040,128]{1,0:T(8,128)S(1)} fusion(f32[1040,128]{1,0:T(8,128)S(1)} %scatter_custom_fusion.2, s32[1024]{0:T(1024)S(1)} %get-tuple-element.17, f32[1024,128]{1,0:T(8,128)S(1)} %convolution_multiply_fusion.2, f32[1024]{0:T(1024)S(1)} %bitcast.90), kind=kCustom, calls=%fused_computation.97 | custom fusion | flops 262144 | bytes 1060864 | tf_op jit(solution)/shard_map/scatter-add | solution.py:128
  219.9 3.5 scatter_fusion
  224.4 5.0 %collective-permute-done.9 = f32[16,33,128]{2,0,1:T(8,128)S(1)} collective-permute-done((f32[16,33,128]{2,0,1:T(8,128)S(1)}, f32[16,33,128]{2,0,1:T(8,128)S(1)}, u32[]{:S(2)}, u32[]{:S(2)}) %collective-permute-start.9) | collective-permute-done | bytes 270368 | tf_op jit(solution)/shard_map/ppermute | solution.py:36
  231.6 39.5 %all-reduce.5.cloned.1.call-done = f32[4,32,16,128]{3,1,2,0:T(8,128)} async-done(((f32[4,32,16,128]{3,1,2,0:T(8,128)}), f32[4,32,16,128]{3,1,2,0:T(8,128)}) %all-reduce.5.cloned.1.call-update) | async-done | bytes 1048592 | tf_op jit(solution)/shard_map/psum | solution.py:179
  281.2 12.7 %collective-permute-done.10 = f32[8,32,4,128]{3,1,2,0:T(8,128)S(1)} collective-permute-done((f32[8,32,4,128]{3,1,2,0:T(8,128)S(1)}, f32[8,32,4,128]{3,1,2,0:T(8,128)S(1)}, u32[]{:S(2)}, u32[]{:S(2)}) %collective-permute-start.10) | collective-permute-done | bytes 524320 | tf_op jit(solution)/shard_map/ppermute | solution.py:24
  293.9 9.3 %collective-permute-done.11 = f32[8,32,4,128]{3,1,2,0:T(8,128)S(1)} collective-permute-done((f32[8,32,4,128]{3,1,2,0:T(8,128)S(1)}, f32[8,32,4,128]{3,1,2,0:T(8,128)S(1)}, u32[]{:S(2)}, u32[]{:S(2)}) %collective-permute-start.11) | collective-permute-done | bytes 524320 | tf_op jit(solution)/shard_map/ppermute | solution.py:26
  303.5 3.7 fusion.87
  318.9 6.8 %collective-permute-done.12 = f32[8,32,24,4]{1,2,3,0:T(8,128)} collective-permute-done((f32[8,32,24,4]{1,2,3,0:T(8,128)}, f32[8,32,24,4]{1,2,3,0:T(8,128)}, u32[]{:S(2)}, u32[]{:S(2)}) %collective-permute-start.12) | collective-permute-done | bytes 98336 | tf_op jit(solution)/shard_map/ppermute | solution.py:24
  325.7 3.6 copy.69
  332.7 5.7 %pad_maximum_fusion.1 = f32[8,32,24,136]{3,1,2,0:T(8,128)S(1)} fusion(f32[8,32,24,4]{3,1,2,0:T(8,128)} %copy.70, f32[8,32,4,128]{3,1,2,0:T(8,128)S(1)} %collective-permute-done.11, f32[8,32,16,128]{3,1,2,0:T(8,128)S(1)} %copy_multiply_fusion, f32[8,32,4,128]{3,1,2,0:T(8,128)S(1)} %collective-permute-done.10, f32[8,32,24,4]{3,1,2,0:T(8,128)} %copy.69), kind=kLoop, calls=%fused_computation.17 | loop fusion | flops 3342336 | bytes 6684672 | tf_op jit(solution)/shard_map/concatenate | solution.py:22
  347.3 6.6 %maximum_select_fusion.2 = f32[8,32,24,136]{3,1,2,0:T(8,128)S(1)} fusion(f32[8,32,20,136]{3,1,2,0:T(8,128)} %slice.405, f32[8,32,4,136]{3,1,2,0:T(8,128)} %rev.24, pred[]{:T(512)S(6)} %eq.20, f32[8,32,24,4]{3,1,2,0:T(8,128)} %copy.70, f32[8,32,4,128]{3,1,2,0:T(8,128)S(1)} %collective-permute-done.11, f32[8,32,16,128]{3,1,2,0:T(8,128)S(1)} %copy_multiply_fusion, ...), kind=kLoop, calls=%fused_computation.18 | loop fusion | flops 5013504 | bytes 10027009 | tf_op jit(solution)/shard_map/jit(_where)/select_n | solution.py:53
  355.2 3.6 broadcast_multiply_fusion
  358.7 12.1 %broadcast_multiply_fusion.1 = (f32[8,32,22,134]{3,1,2,0:T(8,128)}, f32[8,32,22,134]{3,1,2,0:T(8,128)}) fusion(f32[22,134]{1,0:T(8,128)S(1)} %slice_bitcast_fusion.2, f32[8,32,24,136]{3,1,2,0:T(8,128)S(1)} %get-tuple-element.15, f32[8,32,24,136]{3,1,2,0:T(8,128)} %get-tuple-element.16), kind=kLoop, calls=%fused_computation.59 | loop fusion | flops 5282816 | bytes 24161808 | tf_op jit(solution)/shard_map/mul | solution.py:79
  370.8 14.1 %broadcast_multiply_fusion.2 = (f32[8,32,20,132]{3,1,2,0:T(8,128)S(1)}, f32[8,32,20,132]{3,1,2,0:T(8,128)S(1)}) fusion(f32[20,132]{1,0:T(8,128)S(1)} %slice_bitcast_fusion.1, f32[8,32,22,134]{3,1,2,0:T(8,128)} %get-tuple-element.13, f32[8,32,22,134]{3,1,2,0:T(8,128)} %get-tuple-element.14), kind=kLoop, calls=%fused_computation.60 | loop fusion | flops 4730880 | bytes 21637440 | tf_op jit(solution)/shard_map/mul | solution.py:79
  384.9 7.6 %broadcast_multiply_fusion.3 = (f32[8,32,18,130]{3,1,2,0:T(8,128)S(1)}, f32[8,32,18,130]{3,1,2,0:T(8,128)}) fusion(f32[18,130]{1,0:T(8,128)S(1)} %slice_bitcast_fusion, f32[8,32,20,132]{3,1,2,0:T(8,128)S(1)} %get-tuple-element.11, f32[8,32,20,132]{3,1,2,0:T(8,128)S(1)} %get-tuple-element.12), kind=kLoop, calls=%fused_computation.61 | loop fusion | flops 4193280 | bytes 19178640 | tf_op jit(solution)/shard_map/mul | solution.py:79
  392.6 6.8 %bitcast_add_fusion = f32[8,32,16,128]{3,1,2,0:T(8,128)S(1)} fusion(f32[8,32,16,128]{3,2,1,0:T(8,128)S(1)} %copy-done.4, f32[8,32,18,130]{3,1,2,0:T(8,128)S(1)} %get-tuple-element.9, f32[8,32,18,130]{3,1,2,0:T(8,128)} %get-tuple-element.10, s32[32]{0:T(128)S(1)} %copy-done.17, s32[32]{0:T(128)S(1)} %copy-done.15), kind=kOutput, calls=%fused_computation.77 | convolution fusion | flops 205005824 | bytes 16778240 | tf_op jit(solution)/shard_map/lm,klyx->kmyx/dot_general | solution.py:186
  (149 shorter events, 112.6 us)
Async XLA Ops:
  7.2 161.2 %copy-start = (f32[4,32,32]{2,1,0:T(8,128)S(1)}, f32[4,32,32]{2,1,0:T(8,128)}, u32[]{:S(2)}) copy-start(f32[4,32,32]{2,1,0:T(8,128)} %param.21) | copy-start | bytes 49156
  7.2 16.1 %copy-start.9 = (f32[16,128]{1,0:T(8,128)S(1)}, f32[16,128]{1,0:T(8,128)}, u32[]{:S(2)}) copy-start(f32[16,128]{1,0:T(8,128)} %param.19) | copy-start | bytes 24580
  7.2 15.4 %copy-start.19 = (s32[1,2]{1,0:T(1,128)S(1)}, s32[1,2]{1,0:T(1,128)}, u32[]{:S(2)}) copy-start(s32[1,2]{1,0:T(1,128)} %param.22) | copy-start | bytes 28
  7.2 161.2 %all-reduce.3.cloned.1.call-start = ((), (), s32[]{:S(2)}) async-start(), calls=%async_computation | async-start | bytes 2097152 | tf_op jit(solution)/shard_map/psum | solution.py:168
  8.0 15.3 %collective-permute-start.4 = (f32[1,1,4,128]{3,2,1,0:T(4,128)S(1)}, f32[1,1,4,128]{3,2,1,0:T(4,128)S(1)}, u32[]{:S(2)}, u32[]{:S(2)}) collective-permute-start(f32[1,1,4,128]{3,2,1,0:T(4,128)S(1)} %get-tuple-element.47), channel_id=1, source_target_pairs={{0,4},{4,8},{8,12},{12,0},{1,5},{5,9},{9,13},{13,1},{2,6},{6,10},{... | collective-permute-start | bytes 6152 | tf_op jit(solution)/shard_map/ppermute | solution.py:24
  11.0 12.3 %collective-permute-start.5 = (f32[1,1,4,128]{3,2,1,0:T(4,128)S(1)}, f32[1,1,4,128]{3,2,1,0:T(4,128)S(1)}, u32[]{:S(2)}, u32[]{:S(2)}) collective-permute-start(f32[1,1,4,128]{3,2,1,0:T(4,128)S(1)} %get-tuple-element.48), channel_id=1, source_target_pairs={{4,0},{8,4},{12,8},{0,12},{5,1},{9,5},{13,9},{1,13},{6,2},{10,6},{... | collective-permute-start | bytes 6152 | tf_op jit(solution)/shard_map/ppermute | solution.py:26
  13.8 12.8 %copy-start.14 = (s32[32]{0:T(128)}, s32[32]{0:T(128)S(1)}, u32[]{:S(2)}) copy-start(s32[32]{0:T(128)S(1)} %get-tuple-element.61) | copy-start | bytes 388
  13.8 12.8 %copy-start.16 = (s32[32]{0:T(128)}, s32[32]{0:T(128)S(1)}, u32[]{:S(2)}) copy-start(s32[32]{0:T(128)S(1)} %get-tuple-element.62) | copy-start | bytes 388
  18.7 16.8 %collective-permute-start = (f32[8,32,4,128]{3,1,2,0:T(8,128)}, f32[8,32,4,128]{3,1,2,0:T(8,128)S(1)}, u32[]{:S(2)}, u32[]{:S(2)}) collective-permute-start(f32[8,32,4,128]{3,1,2,0:T(8,128)} %get-tuple-element.31), channel_id=1, source_target_pairs={{0,4},{4,8},{8,12},{12,0},{1,5},{5,9},{9,13},{13,1},{2,6},{6,10},{... | collective-permute-start | bytes 1572872 | tf_op jit(solution)/shard_map/ppermute | solution.py:24
  18.7 24.8 %collective-permute-start.1 = (f32[8,32,4,128]{3,1,2,0:T(8,128)}, f32[8,32,4,128]{3,1,2,0:T(8,128)S(1)}, u32[]{:S(2)}, u32[]{:S(2)}) collective-permute-start(f32[8,32,4,128]{3,1,2,0:T(8,128)} %get-tuple-element.32), channel_id=1, source_target_pairs={{4,0},{8,4},{12,8},{0,12},{5,1},{9,5},{13,9},{1,13},{6,2},{10,6},{... | collective-permute-start | bytes 1572872 | tf_op jit(solution)/shard_map/ppermute | solution.py:26
  23.4 3.1 collective-permute-start.6
  23.4 3.1 collective-permute-start.7
  54.3 15.2 %collective-permute-start.3 = (f32[8,32,24,4]{1,2,3,0:T(8,128)}, f32[8,32,24,4]{1,2,3,0:T(8,128)}, u32[]{:S(2)}, u32[]{:S(2)}) collective-permute-start(f32[8,32,24,4]{1,2,3,0:T(8,128)} %copy.53), channel_id=1, source_target_pairs={{1,0},{2,1},{3,2},{0,3},{5,4},{6,5},{7,6},{4,7},{9,8},{10,9},{11,1... | collective-permute-start | bytes 294920 | tf_op jit(solution)/shard_map/ppermute | solution.py:26
  54.4 11.8 %collective-permute-start.2 = (f32[8,32,24,4]{1,2,3,0:T(8,128)}, f32[8,32,24,4]{1,2,3,0:T(8,128)}, u32[]{:S(2)}, u32[]{:S(2)}) collective-permute-start(f32[8,32,24,4]{1,2,3,0:T(8,128)} %copy.52), channel_id=1, source_target_pairs={{0,1},{1,2},{2,3},{3,0},{4,5},{5,6},{6,7},{7,4},{8,9},{9,10},{10,1... | collective-permute-start | bytes 294920 | tf_op jit(solution)/shard_map/ppermute | solution.py:24
  126.8 2.9 copy-start.18
  126.8 3.0 copy-start.13
  126.9 41.5 %copy-start.6 = (f32[4,32,16,128]{3,2,1,0:T(8,128)S(1)}, f32[4,32,16,128]{3,2,1,0:T(8,128)}, u32[]{:S(2)}) copy-start(f32[4,32,16,128]{3,2,1,0:T(8,128)} %param.18) | copy-start | bytes 3145732
  129.0 142.0 %all-reduce.5.cloned.1.call-start = ((), (), s32[]{:S(2)}) async-start(), calls=%async_computation.1 | async-start | bytes 2097152 | tf_op jit(solution)/shard_map/psum | solution.py:179
  171.8 3.8 collective-permute-start.8
  176.4 13.2 %copy-start.8 = (bf16[1024,128]{1,0:T(8,128)(2,1)S(1)}, bf16[1024,128]{1,0:T(8,128)(2,1)}, u32[]{:S(2)}) copy-start(bf16[1024,128]{1,0:T(8,128)(2,1)} %param.25) | copy-start | bytes 786436
  176.7 14.3 %copy-start.10 = (f32[8,1024]{1,0:T(8,128)S(1)}, f32[8,1024]{1,0:T(8,128)}, u32[]{:S(2)}) copy-start(f32[8,1024]{1,0:T(8,128)} %param.27) | copy-start | bytes 98308
  176.7 14.3 %copy-start.11 = (f32[8,1024]{1,0:T(8,128)S(1)}, f32[8,1024]{1,0:T(8,128)}, u32[]{:S(2)}) copy-start(f32[8,1024]{1,0:T(8,128)} %param.26) | copy-start | bytes 98308
  176.7 14.3 %copy-start.12 = (f32[8,128]{1,0:T(8,128)S(1)}, f32[8,128]{1,0:T(8,128)}, u32[]{:S(2)}) copy-start(f32[8,128]{1,0:T(8,128)} %param.28) | copy-start | bytes 12292
  223.4 6.1 %collective-permute-start.9 = (f32[16,33,128]{2,0,1:T(8,128)S(1)}, f32[16,33,128]{2,0,1:T(8,128)S(1)}, u32[]{:S(2)}, u32[]{:S(2)}) collective-permute-start(f32[16,33,128]{2,0,1:T(8,128)S(1)} %slice.398), channel_id=1, source_target_pairs={{0,1},{1,2},{2,3},{3,0},{4,5},{5,6},{6,7},{7,4},{8,9},{9,10},{10,1... | collective-permute-start | bytes 811016 | tf_op jit(solution)/shard_map/ppermute | solution.py:36
  277.2 16.7 %collective-permute-start.10 = (f32[8,32,4,128]{3,1,2,0:T(8,128)S(1)}, f32[8,32,4,128]{3,1,2,0:T(8,128)S(1)}, u32[]{:S(2)}, u32[]{:S(2)}) collective-permute-start(f32[8,32,4,128]{3,1,2,0:T(8,128)S(1)} %get-tuple-element.29), channel_id=1, source_target_pairs={{0,4},{4,8},{8,12},{12,0},{1,5},{5,9},{9,13},{13,1},{2,6},{6,10},{... | collective-permute-start | bytes 1572872 | tf_op jit(solution)/shard_map/ppermute | solution.py:24
  278.7 24.5 %collective-permute-start.11 = (f32[8,32,4,128]{3,1,2,0:T(8,128)S(1)}, f32[8,32,4,128]{3,1,2,0:T(8,128)S(1)}, u32[]{:S(2)}, u32[]{:S(2)}) collective-permute-start(f32[8,32,4,128]{3,1,2,0:T(8,128)S(1)} %get-tuple-element.30), channel_id=1, source_target_pairs={{4,0},{8,4},{12,8},{0,12},{5,1},{9,5},{13,9},{1,13},{6,2},{10,6},{... | collective-permute-start | bytes 1572872 | tf_op jit(solution)/shard_map/ppermute | solution.py:26
  314.0 15.4 %collective-permute-start.13 = (f32[8,32,24,4]{1,2,3,0:T(8,128)}, f32[8,32,24,4]{1,2,3,0:T(8,128)}, u32[]{:S(2)}, u32[]{:S(2)}) collective-permute-start(f32[8,32,24,4]{1,2,3,0:T(8,128)} %copy.68), channel_id=1, source_target_pairs={{1,0},{2,1},{3,2},{0,3},{5,4},{6,5},{7,6},{4,7},{9,8},{10,9},{11,1... | collective-permute-start | bytes 294920 | tf_op jit(solution)/shard_map/ppermute | solution.py:26
  314.5 11.3 %collective-permute-start.12 = (f32[8,32,24,4]{1,2,3,0:T(8,128)}, f32[8,32,24,4]{1,2,3,0:T(8,128)}, u32[]{:S(2)}, u32[]{:S(2)}) collective-permute-start(f32[8,32,24,4]{1,2,3,0:T(8,128)} %copy.67), channel_id=1, source_target_pairs={{0,1},{1,2},{2,3},{3,0},{4,5},{5,6},{6,7},{7,4},{8,9},{9,10},{10,1... | collective-permute-start | bytes 294920 | tf_op jit(solution)/shard_map/ppermute | solution.py:24
  384.9 7.7 %copy-start.4 = (f32[8,32,16,128]{3,2,1,0:T(8,128)S(1)}, f32[8,32,16,128]{3,2,1,0:T(8,128)}, u32[]{:S(2)}) copy-start(f32[8,32,16,128]{3,2,1,0:T(8,128)} %param.16) | copy-start | bytes 6291460
  384.9 7.7 %copy-start.15 = (s32[32]{0:T(128)S(1)}, s32[32]{0:T(128)}, u32[]{:S(2)}) copy-start(s32[32]{0:T(128)} %copy-done.14) | copy-start | bytes 388
  384.9 7.7 %copy-start.17 = (s32[32]{0:T(128)S(1)}, s32[32]{0:T(128)}, u32[]{:S(2)}) copy-start(s32[32]{0:T(128)} %copy-done.16) | copy-start | bytes 388
  392.6 9.3 %copy-start.1 = (f32[4,32,32]{2,1,0:T(8,128)S(1)}, f32[4,32,32]{2,1,0:T(8,128)}, u32[]{:S(2)}) copy-start(f32[4,32,32]{2,1,0:T(8,128)} %param.21) | copy-start | bytes 49156
  (4 other events, 8.8 us)
Sparse Core Ops, SparseCore 0:
  129.1 39.1 all-reduce.2
  231.7 39.3 all-reduce.4
where the time goes:
time: 414 us; the launch traced here: 409 us
  waiting for transfers between devices  142 us (34%)
  other arithmetic  126 us (30%)
  local copies, waits for them, and re-layouts  88.8 us (21%)
  starting transfers between devices  18 us (4%)
  matrix products  17.5 us (4%)
  between operations  16.3 us (4%)
    ppermute x6, waiting for transfers between devices, padded_2(): lax.ppermute(tail, axis, [(i, (i + 1) % count) for i in range(count)])  39.6 us
    psum x1, waiting for transfers between devices, body(): gradient_cells = lax.psum(tile_grad, 'mem')  39.5 us
    psum x1, waiting for transfers between devices, body(): member_total = lax.psum(partial_sum, 'mem')  38.5 us
    mul x4, other arithmetic, sweep_adjoint(): stencil_sum = stencil_of(kappa_pad * padded)  37.3 us
    scatter-add x4, other arithmetic, observe(): returned.at[cell_index[corner]]  27 us
    add x4, other arithmetic, sweep_forward(): padded = padded[:, :, 1:-1, 1:-1] + kappa_pad * stencil_sum  19.2 us
    ppermute x6, waiting for transfers between devices, padded_2(): lax.ppermute(head, axis, [((i + 1) % count, i) for i in range(count)])  17.4 us
    slice x8, local copies, waits for them, and re-layouts, padded_2(): lax.slice_in_dim(cells, cells.shape[dim] - width, cells.shape[dim], axis=...  16.1 us
  transfers between devices with their start and end apart: 16, of which 11 were waited for; matrix products, arithmetic and copies ran while one was open for 5% of the time, Pallas kernels for 0%

commit v1 on v0

v1 whole, which is shorter than its diff:
```python
import math

import jax
import jax.numpy as jnp
from jax import lax
from jax.experimental import pallas as pl
from jax.experimental.pallas import tpu as pltpu
from jax.sharding import PartitionSpec as P

NDIFF = 4

ensemble_weight = 0.8
static_weight = 0.6
vertical_scale = 2.0
highest = lax.Precision.HIGHEST
f32 = jnp.float32
bf16 = jnp.bfloat16
NT = (((1,), (1,)), ((), ()))
TN = (((0,), (0,)), ((), ()))


def shifted(value, axis, steps):
    count = lax.axis_size(axis)
    pairs = [(source, (source + steps) % count) for source in range(count)]
    return lax.ppermute(value, axis, pairs)


def vertical_matrix(vert_bounds, levels):
    row_level = lax.broadcasted_iota(jnp.int32, (levels, levels), 0)
    col_level = lax.broadcasted_iota(jnp.int32, (levels, levels), 1)
    inside = (col_level >= vert_bounds[0][:, None]) & (col_level <= vert_bounds[1][:, None])
    distance = jnp.abs(row_level - col_level).astype(f32)
    return jnp.where(inside, jnp.exp(-distance / vertical_scale), jnp.zeros_like(distance))


def edge_picker(width, depth):
    row = lax.broadcasted_iota(jnp.int32, (2 * depth, width), 0)
    col = lax.broadcasted_iota(jnp.int32, (2 * depth, width), 1)
    return jnp.where(col == jnp.where(row < depth, row, width - 2 * depth + row), 1.0, 0.0)


def params(grid_dims=0):
    if grid_dims:
        return pltpu.CompilerParams(
            dimension_semantics=("arbitrary",) * grid_dims, vmem_limit_bytes=56 << 20
        )
    return pltpu.CompilerParams(vmem_limit_bytes=56 << 20)


def write_edges(tile, rows_ref, cols_ref, rows, depth):
    width = tile(0).shape[1]
    for d in range(depth):
        rows_ref[0, 0, d] = tile(d).astype(bf16)
        rows_ref[1, 0, d] = tile(rows - depth + d).astype(bf16)
    picker = edge_picker(width, depth).astype(bf16)
    stack = jnp.concatenate([tile(y).astype(bf16) for y in range(rows)], axis=0)
    picked = lax.dot_general(picker, stack, NT, preferred_element_type=f32)
    cols_ref[0, 0] = picked[:depth].astype(bf16)
    cols_ref[1, 0] = picked[depth:].astype(bf16)


def pack_kernel(rows, levels, depth, field_ref, rows_ref, cols_ref):
    write_edges(
        lambda y: field_ref[0, pl.ds(y, levels, stride=rows), :], rows_ref, cols_ref, rows, depth
    )


def edge_shapes(members, rows, levels, width, depth):
    shapes = [
        jax.ShapeDtypeStruct((2, members, depth, levels, width), bf16),
        jax.ShapeDtypeStruct((2, members, depth, rows * levels), bf16),
    ]
    specs = [
        pl.BlockSpec((2, 1, depth, levels, width), lambda k: (0, k, 0, 0, 0)),
        pl.BlockSpec((2, 1, depth, rows * levels), lambda k: (0, k, 0, 0)),
    ]
    return shapes, specs


def exchange(row_edges, col_edges, rows, levels, depth):
    gy = lax.axis_size("gy")
    up = [(i, i - 1) for i in range(1, gy)]
    down = [(i, i + 1) for i in range(gy - 1)]
    from_east = shifted(col_edges[0], "gx", -1)
    from_west = shifted(col_edges[1], "gx", 1)
    south = lax.ppermute(row_edges[0], "gy", up)
    north = lax.ppermute(row_edges[1], "gy", down)
    sides = jnp.concatenate([from_east, from_west], axis=1)
    part = depth * levels
    corner_south = lax.ppermute(sides[:, :, :part], "gy", up)
    corner_north = lax.ppermute(sides[:, :, -part:], "gy", down)
    ring = jnp.concatenate([sides, corner_south, corner_north], axis=2)
    return south, north, ring


def kappa_ring(kappa, depth):
    rows, width = kappa.shape
    gy = lax.axis_size("gy")
    turned = kappa.T
    east = shifted(turned[:depth], "gx", -1).T
    west = shifted(turned[-depth:], "gx", 1).T
    wide = jnp.concatenate([kappa, east, jnp.zeros((rows, width - 2 * depth), f32), west], axis=1)
    south = lax.ppermute(wide[:depth], "gy", [(i, i - 1) for i in range(1, gy)])
    north = lax.ppermute(wide[-depth:], "gy", [(i, i + 1) for i in range(gy - 1)])
    return jnp.concatenate([wide, south, north], axis=0)


def fill_ring(tile, south_ref, north_ref, sides_ref, ring, rows, levels, width, depth):
    total = rows + 2 * depth
    for y in range(rows):
        ring[y, :, :width] = tile(y)
    for d in range(depth):
        ring[rows + d, :, :width] = south_ref[0, d].astype(f32)
        ring[rows + depth + d, :, :width] = north_ref[0, d].astype(f32)
    picker = edge_picker(width, depth).astype(bf16)
    side = lax.dot_general(sides_ref[0], picker, TN, preferred_element_type=f32)
    for y in range(total):
        ring[y, :, width:] = side[y * levels : (y + 1) * levels]


def diffuse(ring_a, ring_b, kappa_ref, edge_ref, rows, width, depth, adjoint):
    total = rows + 2 * depth
    at_top = edge_ref[0] == 1
    at_bottom = edge_ref[1] == 1
    source, target = ring_a, ring_b
    for step in range(1, depth + 1):
        wanted = list(range(rows + depth - step)) + list(range(rows + depth + step, total))
        keep = width if step == depth else 2 * width

        def load(y):
            value = source[y]
            return kappa_ref[pl.ds(y, 1), :] * value if adjoint else value

        for y in wanted:
            center = load(y)
            north = load((y - 1) % total)
            south = load((y + 1) % total)
            if y == 0:
                north = jnp.where(at_top, center, north)
            if y == rows - 1:
                south = jnp.where(at_bottom, center, south)
            west = pltpu.roll(center, 1, 1)
            east = pltpu.roll(center, 2 * width - 1, 1)
            change = ((north + south) + (west + east)) - 4.0 * center
            if adjoint:
                result = source[y] + change
            else:
                result = center + kappa_ref[pl.ds(y, 1), :] * change
            target[y, :, :keep] = result[:, :keep]
        source, target = target, source
    return source


def forward_kernel(
    dims, ens_scale, edge_ref, alpha_ref, south_ref, north_ref, sides_ref, kappa_ref, vertical_ref,
    perturb_ref, static_ref, out_ref, ring_a, ring_b, spread, acc,
):
    rows, levels, width, variables, depth = dims
    step = pl.program_id(0)
    fill_ring(
        lambda y: alpha_ref[0, pl.ds(y, levels, stride=rows), :],
        south_ref, north_ref, sides_ref, ring_a, rows, levels, width, depth,
    )
    done = diffuse(ring_a, ring_b, kappa_ref, edge_ref, rows, width, depth, False)
    for y in range(rows):
        spread[pl.ds(y, levels, stride=rows), :] = jnp.dot(
            vertical_ref[...], done[y, :, :width], precision=highest, preferred_element_type=f32
        )

    @pl.when(step == 0)
    def _():
        acc[...] = jnp.zeros_like(acc)

    count = rows * levels
    for v in range(variables):
        acc[v * count : (v + 1) * count] += perturb_ref[0, v].astype(f32) * spread[...]

    @pl.when(step == pl.num_programs(0) - 1)
    def _():
        for y in range(rows):
            column = acc[pl.ds(y, variables * levels, stride=rows), :]
            out_ref[y] = ens_scale * column.T + static_ref[y]


def backward_kernel(
    dims, ens_scale, perturb_ref, grad_ref, main_ref, rows_ref, cols_ref, grad, field,
):
    rows, levels, width, variables, depth = dims

    @pl.when(pl.program_id(0) == 0)
    def _():
        for y in range(rows):
            grad[pl.ds(y, variables * levels, stride=rows), :] = ens_scale * grad_ref[y].T

    count = rows * levels
    total = perturb_ref[0, 0].astype(f32) * grad[:count]
    for v in range(1, variables):
        total = total + perturb_ref[0, v].astype(f32) * grad[v * count : (v + 1) * count]
    field[...] = total
    for y in range(rows):
        main_ref[0, y] = field[pl.ds(y, levels, stride=rows), :]
    write_edges(
        lambda y: field[pl.ds(y, levels, stride=rows), :], rows_ref, cols_ref, rows, depth
    )


def adjoint_kernel(
    dims, edge_ref, alpha_ref, main_ref, south_ref, north_ref, sides_ref, kappa_ref, vertical_ref,
    out_ref, ring_a, ring_b,
):
    rows, levels, width, variables, depth = dims
    fill_ring(
        lambda y: main_ref[0, y],
        south_ref, north_ref, sides_ref, ring_a, rows, levels, width, depth,
    )
    done = diffuse(ring_a, ring_b, kappa_ref, edge_ref, rows, width, depth, True)
    for y in range(rows):
        out_ref[0, pl.ds(y, levels, stride=rows), :] = alpha_ref[
            0, pl.ds(y, levels, stride=rows), :
        ] + jnp.dot(
            vertical_ref[...], done[y, :, :width], precision=highest, preferred_element_type=f32
        )


def split(value):
    high = value.astype(bf16)
    return high, (value - high.astype(f32)).astype(bf16)


def observe_kernel(
    rows, band, padded, count_ref, table_ref, anchor_ref, weight_ref, background_ref, observed_ref,
    inv_var_ref, jacobian_ref, out_ref, high_ref, low_ref,
):
    places = anchor_ref.shape[1]
    anchor = anchor_ref[...]
    anchor_row = anchor // band
    anchor_col = anchor - anchor_row * band
    slot = lax.broadcasted_iota(jnp.int32, (padded, places), 0)
    at_left = slot == anchor_col
    at_right = slot == anchor_col + 1
    total = background_ref[...].astype(f32).T
    for y in range(rows):
        upper = anchor_row == y
        lower = anchor_row == y - 1
        zero = jnp.zeros(anchor.shape, f32)
        left = jnp.where(upper, weight_ref[0:1], jnp.where(lower, weight_ref[2:3], zero))
        right = jnp.where(upper, weight_ref[1:2], jnp.where(lower, weight_ref[3:4], zero))
        weights = jnp.where(at_left, left, jnp.where(at_right, right, 0.0))
        high, low = split(weights)
        high_ref[y] = high
        low_ref[y] = low
        cells = table_ref[y]
        total = total + lax.dot_general(cells, high, TN, preferred_element_type=f32)
        total = total + lax.dot_general(cells, low, TN, preferred_element_type=f32)
    bent = jnp.tanh(total)
    modeled = jnp.dot(jacobian_ref[...], bent, precision=highest, preferred_element_type=f32)
    position = lax.broadcasted_iota(jnp.int32, modeled.shape, 1)
    misfit = jnp.where(
        position < count_ref[0], (modeled - observed_ref[...]) * inv_var_ref[...], 0.0
    )
    back = lax.dot_general(
        jacobian_ref[...], misfit, TN, precision=highest, preferred_element_type=f32
    )
    state_high, state_low = split((1.0 - bent * bent) * back)
    for y in range(rows):
        high = high_ref[y]
        cells = lax.dot_general(high, state_high, NT, preferred_element_type=f32)
        cells = cells + lax.dot_general(low_ref[y], state_high, NT, preferred_element_type=f32)
        cells = cells + lax.dot_general(high, state_low, NT, preferred_element_type=f32)
        out_ref[y] = cells


def choose(index, options):
    result = options[0]
    for place in range(1, len(options)):
        result = jnp.where(index == place, options[place], result)
    return result


def body(
    alpha, perturb, chi, kappa, vert_bounds, static_vert, fine_owner, obs_stencil, obs_weight,
    background, observed, inv_var, jacobian, obs_count,
):
    members, levels, rows, width = alpha.shape
    variables = perturb.shape[1]
    column = variables * levels
    depth = NDIFF
    groups = lax.axis_size("mem")
    band = width // groups
    shift = band // 2
    rim = shift + 1
    me = lax.axis_index("mem")
    count = rows * levels
    places = obs_stencil.shape[0]
    dims = (rows, levels, width, variables, depth)
    ens_scale = ensemble_weight / math.sqrt(members * groups - 1)
    gy_place = lax.axis_index("gy")
    edge = jnp.stack([gy_place == 0, gy_place == lax.axis_size("gy") - 1]).astype(jnp.int32)
    owners = fine_owner[0]
    band_ids = lax.iota(jnp.int32, groups)

    def band_of(group):
        return jnp.sum(jnp.where(owners == group, band_ids, 0))

    smem = pl.BlockSpec(memory_space=pltpu.SMEM)
    vmem = pl.BlockSpec(memory_space=pltpu.VMEM)
    member_block = pl.BlockSpec((1, count, width), lambda k: (k, 0, 0))
    row_block = pl.BlockSpec((1, depth, levels, width), lambda k: (k, 0, 0, 0))
    side_block = pl.BlockSpec((1, 2 * depth, (rows + 2 * depth) * levels), lambda k: (k, 0, 0))
    perturb_block = pl.BlockSpec((1, variables, count, width), lambda k: (k, 0, 0, 0))
    ring_scratch = pltpu.VMEM((rows + 2 * depth, levels, 2 * width), f32)
    edge_out, edge_specs = edge_shapes(members, rows, levels, width, depth)

    alpha_flat = alpha.reshape(members, count, width)
    perturb_flat = perturb.reshape(members, variables, count, width)
    vertical = vertical_matrix(vert_bounds, levels)

    row_edges, col_edges = pl.pallas_call(
        lambda *refs: pack_kernel(rows, levels, depth, *refs),
        grid=(members,),
        in_specs=[member_block],
        out_specs=edge_specs,
        out_shape=edge_out,
        compiler_params=params(1),
        name="pack",
    )(alpha_flat)
    south, north, sides = exchange(row_edges, col_edges, rows, levels, depth)
    kappa_all = kappa_ring(kappa, depth)

    static = jnp.einsum("vlm,vmyx->yxvl", static_vert, chi, precision=highest)
    static = jnp.where(me == 0, static_weight * static, 0.0).reshape(rows, width, column)
    partial = pl.pallas_call(
        lambda *refs: forward_kernel(dims, ens_scale, *refs),
        grid=(members,),
        in_specs=[
            smem, member_block, row_block, row_block, side_block, vmem, vmem, perturb_block, vmem,
        ],
        out_specs=pl.BlockSpec((rows, width, column), lambda k: (0, 0, 0)),
        out_shape=jax.ShapeDtypeStruct((rows, width, column), f32),
        scratch_shapes=[
            ring_scratch,
            ring_scratch,
            pltpu.VMEM((count, width), f32),
            pltpu.VMEM((variables * count, width), f32),
        ],
        compiler_params=params(1),
        name="forward",
    )(edge, alpha_flat, south, north, sides, kappa_all, vertical, perturb_flat, static)

    east_rim = shifted(partial[:, :rim].astype(bf16), "gx", -1)
    wide = jnp.concatenate([partial, east_rim.astype(f32)], axis=1)
    regions = [wide[:, b * band + shift : b * band + shift + band + 1] for b in range(groups)]
    own_band = band_of(me)
    increment = choose(own_band, regions)
    for hop in range(1, groups):
        away = choose(band_of((me + hop) % groups), regions).astype(bf16)
        increment = increment + shifted(away, "mem", hop).astype(f32)
    padded = -(-(band + 1) // 16) * 16
    table = jnp.pad(increment.astype(bf16), ((0, 0), (0, padded - band - 1), (0, 0)))

    region_grad = pl.pallas_call(
        lambda *refs: observe_kernel(rows, band, padded, *refs),
        in_specs=[smem] + [vmem] * 7,
        out_specs=vmem,
        out_shape=jax.ShapeDtypeStruct((rows, padded, column), f32),
        scratch_shapes=[
            pltpu.VMEM((rows, padded, places), bf16),
            pltpu.VMEM((rows, padded, places), bf16),
        ],
        compiler_params=params(),
        name="observe",
    )(
        obs_count, table, obs_stencil.reshape(1, places), obs_weight, background, observed,
        inv_var, jacobian,
    )

    region_grad = region_grad[:, : band + 1]
    pieces = [(own_band, region_grad)]
    for hop in range(1, groups):
        pieces.append((band_of((me - hop) % groups), shifted(region_grad, "mem", hop)))
    wide_grad = jnp.zeros((rows, width + rim, column), f32)
    for b in range(groups):
        placed = choose_equal(b, pieces)
        before = b * band + shift
        after = width + rim - before - band - 1
        wide_grad = wide_grad + jnp.pad(placed, ((0, 0), (before, after), (0, 0)))
    west_rim = shifted(wide_grad[:, width:], "gx", 1)
    grad_cells = wide_grad[:, :width] + jnp.pad(west_rim, ((0, 0), (0, width - rim), (0, 0)))

    main, row_edges, col_edges = pl.pallas_call(
        lambda *refs: backward_kernel(dims, ens_scale, *refs),
        grid=(members,),
        in_specs=[perturb_block, vmem],
        out_specs=[pl.BlockSpec((1, rows, levels, width), lambda k: (k, 0, 0, 0))] + edge_specs,
        out_shape=[jax.ShapeDtypeStruct((members, rows, levels, width), f32)] + edge_out,
        scratch_shapes=[
            pltpu.VMEM((variables * count, width), f32),
            pltpu.VMEM((count, width), f32),
        ],
        compiler_params=params(1),
        name="backward",
    )(perturb_flat, grad_cells)
    south, north, sides = exchange(row_edges, col_edges, rows, levels, depth)
    grad_chi = chi + static_weight * jnp.einsum(
        "vlm,yxvl->vmyx",
        static_vert,
        grad_cells.reshape(rows, width, variables, levels),
        precision=highest,
    )
    grad_alpha = pl.pallas_call(
        lambda *refs: adjoint_kernel(dims, *refs),
        grid=(members,),
        in_specs=[
            smem, member_block, pl.BlockSpec((1, rows, levels, width), lambda k: (k, 0, 0, 0)),
            row_block, row_block, side_block, vmem, vmem,
        ],
        out_specs=member_block,
        out_shape=jax.ShapeDtypeStruct((members, count, width), f32),
        scratch_shapes=[ring_scratch, ring_scratch],
        compiler_params=params(1),
        name="adjoint",
    )(edge, alpha_flat, main, south, north, sides, kappa_all, vertical.T)
    return (grad_alpha.reshape(alpha.shape), grad_chi)


def choose_equal(wanted, pieces):
    result = pieces[0][1]
    for index, piece in pieces[1:]:
        result = jnp.where(index == wanted, piece, result)
    return result


def solution(mesh):
    in_specs = (
        P("mem", None, "gy", "gx"),
        P("mem", None, None, "gy", "gx"),
        P(None, None, "gy", "gx"),
        P("gy", "gx"),
        P(),
        P(),
        P(("gy", "gx"), None),
        P(("mem", "gy", "gx")),
        P(None, ("mem", "gy", "gx")),
        P(("mem", "gy", "gx"), None),
        P(None, ("mem", "gy", "gx")),
        P(None, ("mem", "gy", "gx")),
        P(),
        P(("mem", "gy", "gx")),
    )
    out_specs = (P("mem", None, "gy", "gx"), P(None, None, "gy", "gx"))
    return jax.shard_map(body, mesh=mesh, in_specs=in_specs, out_specs=out_specs, check_vma=False)
```

time: 414 us -> 151 us (0.36)
  other arithmetic: 126 us -> 6.8 us
  waiting for transfers between devices: 142 us -> 28.4 us
  local copies, waits for them, and re-layouts: 88.8 us -> 14 us
  Pallas kernels: 0 us -> 57.9 us
  starting transfers between devices: 18 us -> 35.9 us
  matrix products: 17.5 us -> 2.73 us
  between operations: 16.3 us -> 4.25 us
    psum x2 -> x0, waiting for transfers between devices: 78 us -> none  [the longest x1 39.5 us: body(): gradient_cells = lax.psum(tile_grad, 'mem')]
    pallas_call x0 -> x5, Pallas kernels: none -> 57.9 us  [the longest x1 18.2 us: body(): pl.pallas_call(lambda *refs: forward_kernel(dims, ens_scale, *refs), grid...]
    ppermute x12 -> x10, waiting for transfers between devices: 57 us -> 2.11 us  [the longest x1 1.35 us: kappa_ring(): south = lax.ppermute(wide[:depth], 'gy', [(i, i - 1) for i in range(1, gy)])]
    mul x5 -> x0, other arithmetic: 38.1 us -> none  [the longest x4 37.3 us: sweep_adjoint(): stencil_sum = stencil_of(kappa_pad * padded)]
    slice x21 -> x4, local copies, waits for them, and re-layouts: 35.1 us -> 3.24 us  [the longest x2 1.28 us: body(): region_grad = region_grad[:, :band + 1]]
    scatter-add x5 -> x0, other arithmetic: 30.4 us -> none  [the longest x4 27 us: observe(): returned.at[cell_index[corner]]]
    ppermute x2 -> x10, waiting for transfers between devices: 7.43 us -> 26.3 us  [shifted(): return lax.ppermute(value, axis, pairs)]
    select_n x10 -> x2, other arithmetic: 19.6 us -> 0.86 us  [the longest x1 0.68 us: vertical_matrix(): jnp.where(inside, jnp.exp(-distance / vertical_scale), jnp.zeros_like(dis...]
  transfers between devices with their start and end apart: 16 -> 20, of which waited for: 11 -> 6; matrix products, arithmetic and copies ran while one was open for 5% -> 9% of each run, Pallas kernels for 0% -> 4%
where the time goes in v1:
time: 151 us; the launch traced here: 150 us
  Pallas kernels  57.9 us (38%)
  starting transfers between devices  35.9 us (24%)
  waiting for transfers between devices  28.4 us (19%)
  local copies, waits for them, and re-layouts  14 us (9%)
  other arithmetic  6.8 us (5%)
  between operations  4.25 us (3%)
  matrix products  2.73 us (2%)
    ppermute x10, waiting for transfers between devices, shifted(): return lax.ppermute(value, axis, pairs)  26.3 us
    pallas_call x1, Pallas kernels, body(): pl.pallas_call(lambda *refs: forward_kernel(dims, ens_scale, *refs), grid...  18.2 us
    pallas_call x1, Pallas kernels, body(): pl.pallas_call(lambda *refs: adjoint_kernel(dims, *refs), grid=(members,)...  16.3 us
    pallas_call x1, Pallas kernels, body(): pl.pallas_call(lambda *refs: observe_kernel(rows, band, padded, *refs), i...  9.44 us
    ppermute x2, starting transfers between devices, exchange(): corner_north = lax.ppermute(sides[:, :, -part:], 'gy', down)  8.64 us
    ppermute x10, starting transfers between devices, shifted(): return lax.ppermute(value, axis, pairs)  7.97 us
    pallas_call x1, Pallas kernels, body(): pl.pallas_call(lambda *refs: backward_kernel(dims, ens_scale, *refs), gri...  7.93 us
    ppermute x2, starting transfers between devices, exchange(): north = lax.ppermute(row_edges[1], 'gy', down)  7.71 us
  transfers between devices with their start and end apart: 20, of which 6 were waited for; matrix products, arithmetic and copies ran while one was open for 9% of the time, Pallas kernels for 4%

profile of v1, /device:TPU:0, one launch (start us, length us, event | category | flops | bytes accessed | tf_op | source)
XLA Modules:
  0.0 150.0 jit_solution(12447514749569714427)
XLA Ops:
  1.5 2.4 %collective-permute-start.6 = (f32[4,16]{0,1:T(8,128)S(1)}, f32[4,16]{0,1:T(8,128)S(1)}, u32[]{:S(2)}, u32[]{:S(2)}) collective-permute-start(f32[4,16]{0,1:T(8,128)S(1)} %get-tuple-element.37), channel_id=1, source_target_pairs={{0,3},{1,0},{2,1},{3,2},{4,7},{5,4},{6,5},{7,6},{8,11},{9,8},{10,9... | collective-permute-start | bytes 776 | tf_op jit(solution)/shard_map/ppermute | solution.py:25
  4.0 6.0 %pack.1 = (bf16[2,8,4,32,128]{4,3,2,1,0:T(8,128)(2,1)}, bf16[2,8,4,512]{3,2,1,0:T(4,128)(2,1)}) custom-call(f32[8,512,128]{2,1,0:T(8,128)} %bitcast.59), custom_call_target="tpu_custom_call" | custom-call | tf_op jit(solution)/shard_map/pack/pallas_call | solution.py:318
  10.8 1.8 %collective-permute-start.2 = (bf16[8,4,512]{2,1,0:T(4,128)(2,1)S(1)}, bf16[8,4,512]{2,1,0:T(4,128)(2,1)S(1)}, u32[]{:S(2)}, u32[]{:S(2)}) collective-permute-start(bf16[8,4,512]{2,1,0:T(4,128)(2,1)S(1)} %get-tuple-element.33), channel_id=1, source_target_pairs={{0,3},{1,0},{2,1},{3,2},{4,7},{5,4},{6,5},{7,6},{8,11},{9,8},{10,9... | collective-permute-start | bytes 98312 | tf_op jit(solution)/shard_map/ppermute | solution.py:25
  13.6 3.5 %collective-permute-start.1 = (bf16[8,4,32,128]{3,2,1,0:T(8,128)(2,1)S(1)}, bf16[8,4,32,128]{3,2,1,0:T(8,128)(2,1)S(1)}, u32[]{:S(2)}, u32[]{:S(2)}) collective-permute-start(bf16[8,4,32,128]{3,2,1,0:T(8,128)(2,1)S(1)} %get-tuple-element.25), channel_id=1, source_target_pairs={{0,4},{4,8},{8,12},{1,5},{5,9},{9,13},{2,6},{6,10},{10,14},{3,7},{... | collective-permute-start | bytes 786440 | tf_op jit(solution)/shard_map/ppermute | solution.py:87
  17.9 1.4 fusion.3
  20.0 1.3 copy.32.refs_8_
  21.3 1.3 collective-permute-start
  22.7 1.3 collective-permute-start.8
  24.0 5.2 %collective-permute-start.9 = (f32[4,256]{1,0:T(4,128)S(1)}, f32[4,256]{1,0:T(4,128)S(1)}, u32[]{:S(2)}, u32[]{:S(2)}) collective-permute-start(f32[4,256]{1,0:T(4,128)S(1)} %get-tuple-element.36), channel_id=1, source_target_pairs={{0,4},{4,8},{8,12},{1,5},{5,9},{9,13},{2,6},{6,10},{10,14},{3,7},{... | collective-permute-start | bytes 12296 | tf_op jit(solution)/shard_map/ppermute | solution.py:104
  29.2 1.3 collective-permute-start.4
  30.5 1.4 collective-permute-done.8
  31.9 3.5 %collective-permute-start.5 = (bf16[8,8,128]{2,1,0:T(8,128)(2,1)S(1)}, bf16[8,8,128]{2,1,0:T(8,128)(2,1)S(1)}, u32[]{:S(2)}, u32[]{:S(2)}) collective-permute-start(bf16[8,8,128]{2,1,0:T(8,128)(2,1)S(1)} %get-tuple-element.32), channel_id=1, source_target_pairs={{0,4},{4,8},{8,12},{1,5},{5,9},{9,13},{2,6},{6,10},{10,14},{3,7},{... | collective-permute-start | bytes 49160 | tf_op jit(solution)/shard_map/ppermute | solution.py:91
  38.3 18.2 %forward.1 = f32[16,128,128]{2,1,0:T(8,128)} custom-call(s32[2]{0:T(128)} %add_convert_fusion.1.refs_0_, f32[8,512,128]{2,1,0:T(8,128)} %bitcast.60, bf16[8,4,32,128]{3,2,1,0:T(8,128)(2,1)} %copy-done.8, bf16[8,4,32,128]{3,2,1,0:T(8,128)(2,1)} %copy-done.7, bf16[8,8,768]{2,1,0:T(8,128)(2,1)} %pad_maximum_fusion.1.refs_4_, ...), custom_call_target="tpu_custom_call" | custom-call | tf_op jit(solution)/shard_map/forward/pallas_call | solution.py:332
  59.0 1.4 collective-permute-done.10
  60.5 1.2 select_convert_fusion
  61.7 1.6 %collective-permute-start.11 = (bf16[16,65,128]{2,1,0:T(8,128)(2,1)S(1)}, bf16[16,65,128]{2,1,0:T(8,128)(2,1)S(1)}, u32[]{:S(2)}, u32[]{:S(2)}) collective-permute-start(bf16[16,65,128]{2,1,0:T(8,128)(2,1)S(1)} %select_convert_fusion), channel_id=1, source_target_pairs={{0,16},{16,0},{1,17},{17,1},{2,18},{18,2},{3,19},{19,3},{4,20},{20... | collective-permute-start | bytes 798728 | tf_op jit(solution)/shard_map/ppermute | solution.py:25
  64.5 7.1 %collective-permute-done.11 = bf16[16,65,128]{2,1,0:T(8,128)(2,1)S(1)} collective-permute-done((bf16[16,65,128]{2,1,0:T(8,128)(2,1)S(1)}, bf16[16,65,128]{2,1,0:T(8,128)(2,1)S(1)}, u32[]{:S(2)}, u32[]{:S(2)}) %collective-permute-start.11) | collective-permute-done | bytes 266272 | tf_op jit(solution)/shard_map/ppermute | solution.py:25
  72.4 9.4 %observe.1 = f32[16,80,128]{2,1,0:T(8,128)} custom-call(s32[1]{0:T(128)S(6)} %copy.52.refs_0_, bf16[16,80,128]{2,1,0:T(8,128)(2,1)} %pad.16.refs_1_, s32[1,1024]{1,0:T(1,128)} %bitcast.72, f32[4,1024]{1,0:T(4,128)} %refs_3_.1, bf16[1024,128]{1,0:T(8,128)(2,1)} %refs_4_.1, f32[8,1024]{1,0:T(8,128)} %refs_5_.1, f32[8,1024]{1,0:T(8,128)} %refs_6_.1, ...), custom_call_target="tpu_custom_call" | custom-call | tf_op jit(solution)/shard_map/observe/pallas_call | solution.py:361
  81.8 1.2 slice.101
  83.1 1.6 %collective-permute-start.12 = (f32[16,65,128]{2,0,1:T(8,128)S(1)}, f32[16,65,128]{2,0,1:T(8,128)S(1)}, u32[]{:S(2)}, u32[]{:S(2)}) collective-permute-start(f32[16,65,128]{2,0,1:T(8,128)S(1)} %copy.33), channel_id=1, source_target_pairs={{0,16},{16,0},{1,17},{17,1},{2,18},{18,2},{3,19},{19,3},{4,20},{20... | collective-permute-start | bytes 1597448 | tf_op jit(solution)/shard_map/ppermute | solution.py:25
  86.1 11.3 %collective-permute-done.12 = f32[16,65,128]{2,0,1:T(8,128)S(1)} collective-permute-done((f32[16,65,128]{2,0,1:T(8,128)S(1)}, f32[16,65,128]{2,0,1:T(8,128)S(1)}, u32[]{:S(2)}, u32[]{:S(2)}) %collective-permute-start.12) | collective-permute-done | bytes 532512 | tf_op jit(solution)/shard_map/ppermute | solution.py:25
  97.6 6.5 %collective-permute-done.13 = f32[16,33,128]{2,1,0:T(8,128)S(1)} collective-permute-done((f32[16,33,128]{2,1,0:T(8,128)S(1)}, f32[16,33,128]{2,1,0:T(8,128)S(1)}, u32[]{:S(2)}, u32[]{:S(2)}) %collective-permute-start.13) | collective-permute-done | bytes 270368 | tf_op jit(solution)/shard_map/ppermute | solution.py:25
  105.2 7.9 %backward.1 = (f32[8,16,32,128]{3,2,1,0:T(8,128)}, bf16[2,8,4,32,128]{4,3,2,1,0:T(8,128)(2,1)}, bf16[2,8,4,512]{3,2,1,0:T(4,128)(2,1)}) custom-call(bf16[8,4,512,128]{3,2,1,0:T(8,128)(2,1)} %bitcast.63, f32[16,128,128]{2,1,0:T(8,128)} %fusion.5.refs_1_), custom_call_target="tpu_custom_call" | custom-call | tf_op jit(solution)/shard_map/backward/pallas_call | solution.py:390
  113.1 1.4 slice_bitcast_fusion.5
  115.1 1.8 %slice_bitcast_fusion = (bf16[8,4,32,128]{3,2,1,0:T(8,128)(2,1)}, bf16[8,4,32,128]{3,2,1,0:T(8,128)(2,1)S(1)}) fusion(bf16[2,8,4,32,128]{4,3,2,1,0:T(8,128)(2,1)} %get-tuple-element.10), kind=kLoop, calls=%fused_computation.19 | loop fusion | bytes 1048576 | tf_op jit(solution)/shard_map/squeeze | solution.py:87
  117.2 4.2 %collective-permute-start.15 = (bf16[8,4,32,128]{3,2,1,0:T(8,128)(2,1)}, bf16[8,4,32,128]{3,2,1,0:T(8,128)(2,1)S(1)}, u32[]{:S(2)}, u32[]{:S(2)}) collective-permute-start(bf16[8,4,32,128]{3,2,1,0:T(8,128)(2,1)} %get-tuple-element.23), channel_id=1, source_target_pairs={{0,4},{4,8},{8,12},{1,5},{5,9},{9,13},{2,6},{6,10},{10,14},{3,7},{... | collective-permute-start | bytes 786440 | tf_op jit(solution)/shard_map/ppermute | solution.py:87
  121.4 1.3 collective-permute-start.14
  122.7 1.3 collective-permute-start.18
  124.0 5.2 %collective-permute-start.19 = (bf16[8,8,128]{2,1,0:T(8,128)(2,1)S(1)}, bf16[8,8,128]{2,1,0:T(8,128)(2,1)S(1)}, u32[]{:S(2)}, u32[]{:S(2)}) collective-permute-start(bf16[8,8,128]{2,1,0:T(8,128)(2,1)S(1)} %get-tuple-element.28), channel_id=1, source_target_pairs={{0,4},{4,8},{8,12},{1,5},{5,9},{9,13},{2,6},{6,10},{10,14},{3,7},{... | collective-permute-start | bytes 49160 | tf_op jit(solution)/shard_map/ppermute | solution.py:91
  129.2 1.3 fusion.1
  130.6 1.6 %copy.40 = f32[4,32,16,128]{3,2,1,0:T(8,128)} copy(f32[4,32,16,128]{3,1,2,0:T(8,128)S(1)} %fusion.1) | data formatting | bytes 2097152
  133.6 16.3 %adjoint.1 = f32[8,512,128]{2,1,0:T(8,128)} custom-call(s32[2]{0:T(128)} %add_convert_fusion.1.refs_0_, f32[8,512,128]{2,1,0:T(8,128)} %bitcast.61, f32[8,16,32,128]{3,2,1,0:T(8,128)} %get-tuple-element.9.refs_2_, bf16[8,4,32,128]{3,2,1,0:T(8,128)(2,1)} %copy-done.6, bf16[8,4,32,128]{3,2,1,0:T(8,128)(2,1)} %copy-done.5, ...), custom_call_target="tpu_custom_call" | custom-call | tf_op jit(solution)/shard_map/adjoint/pallas_call | solution.py:410
  (69 shorter events, 13.7 us)
Async XLA Ops:
  0.6 17.2 %copy-start = (f32[4,32,32]{2,1,0:T(8,128)S(1)}, f32[4,32,32]{2,1,0:T(8,128)}, u32[]{:S(2)}) copy-start(f32[4,32,32]{2,1,0:T(8,128)} %param.19) | copy-start | bytes 49156
  0.6 16.5 %copy-start.10 = (s32[2,32]{1,0:T(2,128)S(1)}, s32[2,32]{1,0:T(2,128)}, u32[]{:S(2)}) copy-start(s32[2,32]{1,0:T(2,128)} %param.18) | copy-start | bytes 772
  0.7 17.2 %copy-start.4 = (f32[4,32,16,128]{3,2,1,0:T(8,128)S(1)}, f32[4,32,16,128]{3,2,1,0:T(8,128)}, u32[]{:S(2)}) copy-start(f32[4,32,16,128]{3,2,1,0:T(8,128)} %param.16) | copy-start | bytes 3145732
  1.5 19.8 %collective-permute-start.6 = (f32[4,16]{0,1:T(8,128)S(1)}, f32[4,16]{0,1:T(8,128)S(1)}, u32[]{:S(2)}, u32[]{:S(2)}) collective-permute-start(f32[4,16]{0,1:T(8,128)S(1)} %get-tuple-element.37), channel_id=1, source_target_pairs={{0,3},{1,0},{2,1},{3,2},{4,7},{5,4},{6,5},{7,6},{8,11},{9,8},{10,9... | collective-permute-start | bytes 776 | tf_op jit(solution)/shard_map/ppermute | solution.py:25
  4.0 18.6 %collective-permute-start.7 = (f32[4,16]{0,1:T(8,128)S(1)}, f32[4,16]{0,1:T(8,128)S(1)}, u32[]{:S(2)}, u32[]{:S(2)}) collective-permute-start(f32[4,16]{0,1:T(8,128)S(1)} %get-tuple-element.38), channel_id=1, source_target_pairs={{0,1},{1,2},{2,3},{3,0},{4,5},{5,6},{6,7},{7,4},{8,9},{9,10},{10,1... | collective-permute-start | bytes 776 | tf_op jit(solution)/shard_map/ppermute | solution.py:25
  10.8 13.2 %collective-permute-start.2 = (bf16[8,4,512]{2,1,0:T(4,128)(2,1)S(1)}, bf16[8,4,512]{2,1,0:T(4,128)(2,1)S(1)}, u32[]{:S(2)}, u32[]{:S(2)}) collective-permute-start(bf16[8,4,512]{2,1,0:T(4,128)(2,1)S(1)} %get-tuple-element.33), channel_id=1, source_target_pairs={{0,3},{1,0},{2,1},{3,2},{4,7},{5,4},{6,5},{7,6},{8,11},{9,8},{10,9... | collective-permute-start | bytes 98312 | tf_op jit(solution)/shard_map/ppermute | solution.py:25
  12.6 16.6 %collective-permute-start.3 = (bf16[8,4,512]{2,1,0:T(4,128)(2,1)S(1)}, bf16[8,4,512]{2,1,0:T(4,128)(2,1)S(1)}, u32[]{:S(2)}, u32[]{:S(2)}) collective-permute-start(bf16[8,4,512]{2,1,0:T(4,128)(2,1)S(1)} %get-tuple-element.34), channel_id=1, source_target_pairs={{0,1},{1,2},{2,3},{3,0},{4,5},{5,6},{6,7},{7,4},{8,9},{9,10},{10,1... | collective-permute-start | bytes 98312 | tf_op jit(solution)/shard_map/ppermute | solution.py:25
  13.6 23.8 %collective-permute-start.1 = (bf16[8,4,32,128]{3,2,1,0:T(8,128)(2,1)S(1)}, bf16[8,4,32,128]{3,2,1,0:T(8,128)(2,1)S(1)}, u32[]{:S(2)}, u32[]{:S(2)}) collective-permute-start(bf16[8,4,32,128]{3,2,1,0:T(8,128)(2,1)S(1)} %get-tuple-element.25), channel_id=1, source_target_pairs={{0,4},{4,8},{8,12},{1,5},{5,9},{9,13},{2,6},{6,10},{10,14},{3,7},{... | collective-permute-start | bytes 786440 | tf_op jit(solution)/shard_map/ppermute | solution.py:87
  19.9 2.7 %copy-start.9 = (f32[16,128]{1,0:T(8,128)S(1)}, f32[16,128]{1,0:T(8,128)}, u32[]{:S(2)}) copy-start(f32[16,128]{1,0:T(8,128)} %param.17) | copy-start | bytes 24580
  21.3 16.2 %collective-permute-start = (bf16[8,4,32,128]{3,2,1,0:T(8,128)(2,1)S(1)}, bf16[8,4,32,128]{3,2,1,0:T(8,128)(2,1)S(1)}, u32[]{:S(2)}, u32[]{:S(2)}) collective-permute-start(bf16[8,4,32,128]{3,2,1,0:T(8,128)(2,1)S(1)} %get-tuple-element.26), channel_id=1, source_target_pairs={{4,0},{8,4},{12,8},{5,1},{9,5},{13,9},{6,2},{10,6},{14,10},{7,3},{... | collective-permute-start | bytes 786440 | tf_op jit(solution)/shard_map/ppermute | solution.py:86
  22.7 9.2 %collective-permute-start.8 = (f32[4,256]{1,0:T(4,128)S(1)}, f32[4,256]{1,0:T(4,128)S(1)}, u32[]{:S(2)}, u32[]{:S(2)}) collective-permute-start(f32[4,256]{1,0:T(4,128)S(1)} %get-tuple-element.35), channel_id=1, source_target_pairs={{4,0},{8,4},{12,8},{5,1},{9,5},{13,9},{6,2},{10,6},{14,10},{7,3},{... | collective-permute-start | bytes 12296 | tf_op jit(solution)/shard_map/ppermute | solution.py:103
  24.0 11.3 %collective-permute-start.9 = (f32[4,256]{1,0:T(4,128)S(1)}, f32[4,256]{1,0:T(4,128)S(1)}, u32[]{:S(2)}, u32[]{:S(2)}) collective-permute-start(f32[4,256]{1,0:T(4,128)S(1)} %get-tuple-element.36), channel_id=1, source_target_pairs={{0,4},{4,8},{8,12},{1,5},{5,9},{9,13},{2,6},{6,10},{10,14},{3,7},{... | collective-permute-start | bytes 12296 | tf_op jit(solution)/shard_map/ppermute | solution.py:104
  29.2 6.8 %collective-permute-start.4 = (bf16[8,8,128]{2,1,0:T(8,128)(2,1)S(1)}, bf16[8,8,128]{2,1,0:T(8,128)(2,1)S(1)}, u32[]{:S(2)}, u32[]{:S(2)}) collective-permute-start(bf16[8,8,128]{2,1,0:T(8,128)(2,1)S(1)} %get-tuple-element.31), channel_id=1, source_target_pairs={{4,0},{8,4},{12,8},{5,1},{9,5},{13,9},{6,2},{10,6},{14,10},{7,3},{... | collective-permute-start | bytes 49160 | tf_op jit(solution)/shard_map/ppermute | solution.py:90
  31.9 4.9 %collective-permute-start.5 = (bf16[8,8,128]{2,1,0:T(8,128)(2,1)S(1)}, bf16[8,8,128]{2,1,0:T(8,128)(2,1)S(1)}, u32[]{:S(2)}, u32[]{:S(2)}) collective-permute-start(bf16[8,8,128]{2,1,0:T(8,128)(2,1)S(1)} %get-tuple-element.32), channel_id=1, source_target_pairs={{0,4},{4,8},{8,12},{1,5},{5,9},{9,13},{2,6},{6,10},{10,14},{3,7},{... | collective-permute-start | bytes 49160 | tf_op jit(solution)/shard_map/ppermute | solution.py:91
  37.5 0.7 copy-start.7
  37.5 0.8 copy-start.8
  38.3 19.4 %copy-start.11 = (s32[1,2]{1,0:T(1,128)S(1)}, s32[1,2]{1,0:T(1,128)}, u32[]{:S(2)}) copy-start(s32[1,2]{1,0:T(1,128)} %param.20) | copy-start | bytes 28
  56.5 15.1 %copy-start.1 = (f32[16,128,128]{2,1,0:T(8,128)S(1)}, f32[16,128,128]{2,1,0:T(8,128)}, u32[]{:S(2)}) copy-start(f32[16,128,128]{2,1,0:T(8,128)} %forward.1) | copy-start | bytes 3145732
  57.6 2.9 %collective-permute-start.10 = (bf16[16,33,128]{2,1,0:T(8,128)(2,1)S(1)}, bf16[16,33,128]{2,1,0:T(8,128)(2,1)S(1)}, u32[]{:S(2)}, u32[]{:S(2)}) collective-permute-start(bf16[16,33,128]{2,1,0:T(8,128)(2,1)S(1)} %slice.127), channel_id=1, source_target_pairs={{0,3},{1,0},{2,1},{3,2},{4,7},{5,4},{6,5},{7,6},{8,11},{9,8},{10,9... | collective-permute-start | bytes 405512 | tf_op jit(solution)/shard_map/ppermute | solution.py:25
  61.7 9.8 %collective-permute-start.11 = (bf16[16,65,128]{2,1,0:T(8,128)(2,1)S(1)}, bf16[16,65,128]{2,1,0:T(8,128)(2,1)S(1)}, u32[]{:S(2)}, u32[]{:S(2)}) collective-permute-start(bf16[16,65,128]{2,1,0:T(8,128)(2,1)S(1)} %select_convert_fusion), channel_id=1, source_target_pairs={{0,16},{16,0},{1,17},{17,1},{2,18},{18,2},{3,19},{19,3},{4,20},{20... | collective-permute-start | bytes 798728 | tf_op jit(solution)/shard_map/ppermute | solution.py:25
  81.8 15.5 %copy-start.3 = (f32[16,80,128]{2,1,0:T(8,128)S(1)}, f32[16,80,128]{2,1,0:T(8,128)}, u32[]{:S(2)}) copy-start(f32[16,80,128]{2,1,0:T(8,128)} %observe.1) | copy-start | bytes 1966084
  83.1 14.2 %collective-permute-start.12 = (f32[16,65,128]{2,0,1:T(8,128)S(1)}, f32[16,65,128]{2,0,1:T(8,128)S(1)}, u32[]{:S(2)}, u32[]{:S(2)}) collective-permute-start(f32[16,65,128]{2,0,1:T(8,128)S(1)} %copy.33), channel_id=1, source_target_pairs={{0,16},{16,0},{1,17},{17,1},{2,18},{18,2},{3,19},{19,3},{4,20},{20... | collective-permute-start | bytes 1597448 | tf_op jit(solution)/shard_map/ppermute | solution.py:25
  97.6 6.6 %collective-permute-start.13 = (f32[16,33,128]{2,1,0:T(8,128)S(1)}, f32[16,33,128]{2,1,0:T(8,128)S(1)}, u32[]{:S(2)}, u32[]{:S(2)}) collective-permute-start(f32[16,33,128]{2,1,0:T(8,128)S(1)} %pad_add_fusion), channel_id=1, source_target_pairs={{0,1},{1,2},{2,3},{3,0},{4,5},{5,6},{6,7},{7,4},{8,9},{9,10},{10,1... | collective-permute-start | bytes 811016 | tf_op jit(solution)/shard_map/ppermute | solution.py:25
  105.2 11.6 %copy-start.2 = (f32[16,128,128]{2,1,0:T(8,128)S(1)}, f32[16,128,128]{2,1,0:T(8,128)}, u32[]{:S(2)}) copy-start(f32[16,128,128]{2,1,0:T(8,128)} %fusion.5.refs_1_) | copy-start | bytes 3145732
  114.5 8.2 %collective-permute-start.16 = (bf16[8,4,512]{2,1,0:T(4,128)(2,1)}, bf16[8,4,512]{2,1,0:T(4,128)(2,1)S(1)}, u32[]{:S(2)}, u32[]{:S(2)}) collective-permute-start(bf16[8,4,512]{2,1,0:T(4,128)(2,1)} %get-tuple-element.29), channel_id=1, source_target_pairs={{0,3},{1,0},{2,1},{3,2},{4,7},{5,4},{6,5},{7,6},{8,11},{9,8},{10,9... | collective-permute-start | bytes 98312 | tf_op jit(solution)/shard_map/ppermute | solution.py:25
  114.5 8.2 %collective-permute-start.17 = (bf16[8,4,512]{2,1,0:T(4,128)(2,1)}, bf16[8,4,512]{2,1,0:T(4,128)(2,1)S(1)}, u32[]{:S(2)}, u32[]{:S(2)}) collective-permute-start(bf16[8,4,512]{2,1,0:T(4,128)(2,1)} %get-tuple-element.30), channel_id=1, source_target_pairs={{0,1},{1,2},{2,3},{3,0},{4,5},{5,6},{6,7},{7,4},{8,9},{9,10},{10,1... | collective-permute-start | bytes 98312 | tf_op jit(solution)/shard_map/ppermute | solution.py:25
  117.2 15.7 %collective-permute-start.15 = (bf16[8,4,32,128]{3,2,1,0:T(8,128)(2,1)}, bf16[8,4,32,128]{3,2,1,0:T(8,128)(2,1)S(1)}, u32[]{:S(2)}, u32[]{:S(2)}) collective-permute-start(bf16[8,4,32,128]{3,2,1,0:T(8,128)(2,1)} %get-tuple-element.23), channel_id=1, source_target_pairs={{0,4},{4,8},{8,12},{1,5},{5,9},{9,13},{2,6},{6,10},{10,14},{3,7},{... | collective-permute-start | bytes 786440 | tf_op jit(solution)/shard_map/ppermute | solution.py:87
  121.4 11.4 %collective-permute-start.14 = (bf16[8,4,32,128]{3,2,1,0:T(8,128)(2,1)S(1)}, bf16[8,4,32,128]{3,2,1,0:T(8,128)(2,1)S(1)}, u32[]{:S(2)}, u32[]{:S(2)}) collective-permute-start(bf16[8,4,32,128]{3,2,1,0:T(8,128)(2,1)S(1)} %get-tuple-element.24), channel_id=1, source_target_pairs={{4,0},{8,4},{12,8},{5,1},{9,5},{13,9},{6,2},{10,6},{14,10},{7,3},{... | collective-permute-start | bytes 786440 | tf_op jit(solution)/shard_map/ppermute | solution.py:86
  122.7 9.4 %collective-permute-start.18 = (bf16[8,8,128]{2,1,0:T(8,128)(2,1)S(1)}, bf16[8,8,128]{2,1,0:T(8,128)(2,1)S(1)}, u32[]{:S(2)}, u32[]{:S(2)}) collective-permute-start(bf16[8,8,128]{2,1,0:T(8,128)(2,1)S(1)} %get-tuple-element.27), channel_id=1, source_target_pairs={{4,0},{8,4},{12,8},{5,1},{9,5},{13,9},{6,2},{10,6},{14,10},{7,3},{... | collective-permute-start | bytes 49160 | tf_op jit(solution)/shard_map/ppermute | solution.py:90
  124.0 8.1 %collective-permute-start.19 = (bf16[8,8,128]{2,1,0:T(8,128)(2,1)S(1)}, bf16[8,8,128]{2,1,0:T(8,128)(2,1)S(1)}, u32[]{:S(2)}, u32[]{:S(2)}) collective-permute-start(bf16[8,8,128]{2,1,0:T(8,128)(2,1)S(1)} %get-tuple-element.28), channel_id=1, source_target_pairs={{0,4},{4,8},{8,12},{1,5},{5,9},{9,13},{2,6},{6,10},{10,14},{3,7},{... | collective-permute-start | bytes 49160 | tf_op jit(solution)/shard_map/ppermute | solution.py:91
  132.8 0.7 copy-start.5
  132.8 0.8 copy-start.6

commit v2 on v1

--- a/solution.py
+++ b/solution.py
@@ -59,10 +59,32 @@
     cols_ref[1, 0] = picked[depth:].astype(bf16)
 
 
-def pack_kernel(rows, levels, depth, field_ref, rows_ref, cols_ref):
-    write_edges(
-        lambda y: field_ref[0, pl.ds(y, levels, stride=rows), :], rows_ref, cols_ref, rows, depth
+def kappa_parts(value, levels):
+    high = value.astype(bf16).astype(f32)
+    middle = (value - high).astype(bf16).astype(f32)
+    low = value - high - middle
+    level = lax.broadcasted_iota(jnp.int32, (levels, value.shape[1]), 0)
+    return jnp.where(
+        level == 0, high, jnp.where(level == 1, middle, jnp.where(level == 2, low, 0.0))
     )
+
+
+def pack_kernel(rows, levels, depth, kappa_ref, field_ref, rows_ref, cols_ref):
+    step = pl.program_id(0)
+    last = pl.num_programs(0) - 1
+
+    @pl.when(step < last)
+    def _():
+        write_edges(
+            lambda y: field_ref[0, pl.ds(y, levels, stride=rows), :],
+            rows_ref, cols_ref, rows, depth,
+        )
+
+    @pl.when(step == last)
+    def _():
+        write_edges(
+            lambda y: kappa_parts(kappa_ref[y : y + 1, :], levels), rows_ref, cols_ref, rows, depth
+        )
 
 
 def edge_shapes(members, rows, levels, width, depth):
@@ -77,45 +99,155 @@
     return shapes, specs
 
 
-def exchange(row_edges, col_edges, rows, levels, depth):
-    gy = lax.axis_size("gy")
-    up = [(i, i - 1) for i in range(1, gy)]
-    down = [(i, i + 1) for i in range(gy - 1)]
-    from_east = shifted(col_edges[0], "gx", -1)
-    from_west = shifted(col_edges[1], "gx", 1)
-    south = lax.ppermute(row_edges[0], "gy", up)
-    north = lax.ppermute(row_edges[1], "gy", down)
-    sides = jnp.concatenate([from_east, from_west], axis=1)
+def exchange_kernel(
+    part, row_ref, col_ref, south, north, east, west, south_east, south_west, north_east,
+    north_west, send, recv,
+):
+    gx, gy = lax.axis_index("gx"), lax.axis_index("gy")
+    gx_count, gy_count = lax.axis_size("gx"), lax.axis_size("gy")
+    to_east = {"gx": lax.rem(gx + 1, gx_count)}
+    to_west = {"gx": lax.rem(gx + gx_count - 1, gx_count)}
+    to_north = {"gy": gy - 1}
+    to_south = {"gy": gy + 1}
+    has_north = gy > 0
+    has_south = gy < gy_count - 1
+    barrier = pltpu.get_barrier_semaphore()
+
+    def greet(device):
+        pl.semaphore_signal(
+            barrier, inc=1, device_id=device, device_id_type=pl.DeviceIdType.MESH
+        )
+
+    def copy(source, target, place, device):
+        return pltpu.make_async_remote_copy(
+            src_ref=source, dst_ref=target, send_sem=send.at[place], recv_sem=recv.at[place],
+            device_id=device, device_id_type=pl.DeviceIdType.MESH,
+        )
+
+    cols = [copy(col_ref.at[0], east, 0, to_west), copy(col_ref.at[1], west, 1, to_east)]
+    lanes = east.shape[2]
+    first, final = pl.ds(0, part), pl.ds(lanes - part, part)
+    up = [
+        copy(row_ref.at[0], south, 2, to_north),
+        copy(east.at[:, :, first], south_east, 4, to_north),
+        copy(west.at[:, :, first], south_west, 5, to_north),
+    ]
+    down = [
+        copy(row_ref.at[1], north, 3, to_south),
+        copy(east.at[:, :, final], north_east, 6, to_south),
+        copy(west.at[:, :, final], north_west, 7, to_south),
+    ]
+    greet(to_east)
+    greet(to_west)
+    pl.when(has_north)(lambda: greet(to_north))
+    pl.when(has_south)(lambda: greet(to_south))
+    peers = 2 + has_north.astype(jnp.int32) + has_south.astype(jnp.int32)
+    pl.semaphore_wait(barrier, peers)
+    for item in cols:
+        item.start()
+    pl.when(has_north)(lambda: up[0].start())
+    pl.when(has_south)(lambda: down[0].start())
+
+    @pl.when(jnp.logical_not(has_north))
+    def _():
+        for item in (north, north_east, north_west):
+            item[...] = jnp.zeros_like(item)
+
+    @pl.when(jnp.logical_not(has_south))
+    def _():
+        for item in (south, south_east, south_west):
+            item[...] = jnp.zeros_like(item)
+
+    for item in cols:
+        item.wait_recv()
+
+    @pl.when(has_north)
+    def _():
+        up[1].start()
+        up[2].start()
+
+    @pl.when(has_south)
+    def _():
+        down[1].start()
+        down[2].start()
+
+    for item in cols:
+        item.wait_send()
+
+    @pl.when(has_north)
+    def _():
+        for item in up:
+            item.wait_send()
+        for item in down:
+            item.wait_recv()
+
+    @pl.when(has_south)
+    def _():
+        for item in down:
+            item.wait_send()
+        for item in up:
+            item.wait_recv()
+
+
+def exchange(row_edges, col_edges, levels, depth, collective):
+    members, lanes = col_edges.shape[1], col_edges.shape[3]
     part = depth * levels
-    corner_south = lax.ppermute(sides[:, :, :part], "gy", up)
-    corner_north = lax.ppermute(sides[:, :, -part:], "gy", down)
-    ring = jnp.concatenate([sides, corner_south, corner_north], axis=2)
-    return south, north, ring
-
-
-def kappa_ring(kappa, depth):
-    rows, width = kappa.shape
-    gy = lax.axis_size("gy")
-    turned = kappa.T
-    east = shifted(turned[:depth], "gx", -1).T
-    west = shifted(turned[-depth:], "gx", 1).T
-    wide = jnp.concatenate([kappa, east, jnp.zeros((rows, width - 2 * depth), f32), west], axis=1)
-    south = lax.ppermute(wide[:depth], "gy", [(i, i - 1) for i in range(1, gy)])
-    north = lax.ppermute(wide[-depth:], "gy", [(i, i + 1) for i in range(gy - 1)])
-    return jnp.concatenate([wide, south, north], axis=0)
-
-
-def fill_ring(tile, south_ref, north_ref, sides_ref, ring, rows, levels, width, depth):
+    row = jax.ShapeDtypeStruct(row_edges.shape[1:], bf16)
+    side = jax.ShapeDtypeStruct((members, depth, lanes), bf16)
+    corner = jax.ShapeDtypeStruct((members, depth, part), bf16)
+    vmem = pl.BlockSpec(memory_space=pltpu.VMEM)
+    return pl.pallas_call(
+        lambda *refs: exchange_kernel(part, *refs),
+        in_specs=[vmem] * 2,
+        out_specs=[vmem] * 8,
+        out_shape=[row, row, side, side, corner, corner, corner, corner],
+        scratch_shapes=[pltpu.SemaphoreType.DMA((8,)), pltpu.SemaphoreType.DMA((8,))],
+        compiler_params=pltpu.CompilerParams(collective_id=collective, has_side_effects=True),
+        name="exchange",
+    )(row_edges, col_edges)
+
+
+def halo_specs(members, rows, levels, width, depth, place):
+    row = pl.BlockSpec((1, depth, levels, width), lambda k: (place(k), 0, 0, 0))
+    side = pl.BlockSpec((1, depth, rows * levels), lambda k: (place(k), 0, 0))
+    corner = pl.BlockSpec((1, depth, depth * levels), lambda k: (place(k), 0, 0))
+    return [row, row, side, side, corner, corner, corner, corner]
+
+
+def side_lanes(halo, width, depth):
+    south, north, east, west, south_east, south_west, north_east, north_west = halo
+    picker = edge_picker(width, depth).astype(bf16)
+    easts = jnp.concatenate([east[0], south_east[0], north_east[0]], axis=1)
+    wests = jnp.concatenate([west[0], south_west[0], north_west[0]], axis=1)
+    return lax.dot_general(
+        easts, picker[:depth], TN, preferred_element_type=f32
+    ) + lax.dot_general(wests, picker[depth:], TN, preferred_element_type=f32)
+
+
+def fill_ring(tile, halo, ring, rows, levels, width, depth):
     total = rows + 2 * depth
     for y in range(rows):
         ring[y, :, :width] = tile(y)
     for d in range(depth):
-        ring[rows + d, :, :width] = south_ref[0, d].astype(f32)
-        ring[rows + depth + d, :, :width] = north_ref[0, d].astype(f32)
-    picker = edge_picker(width, depth).astype(bf16)
-    side = lax.dot_general(sides_ref[0], picker, TN, preferred_element_type=f32)
+        ring[rows + d, :, :width] = halo[0][0, d].astype(f32)
+        ring[rows + depth + d, :, :width] = halo[1][0, d].astype(f32)
+    side = side_lanes(halo, width, depth)
     for y in range(total):
         ring[y, :, width:] = side[y * levels : (y + 1) * levels]
+
+
+def fill_kappa(kappa_ref, halo, out_ref, rows, levels, width, depth):
+    out_ref[:rows, :width] = kappa_ref[...]
+    for d in range(depth):
+        for base, ref in ((rows, halo[0]), (rows + depth, halo[1])):
+            out_ref[base + d : base + d + 1, :width] = jnp.sum(
+                ref[0, d].astype(f32), axis=0, keepdims=True
+            )
+    side = side_lanes(halo, width, depth)
+    for y in range(rows + 2 * depth):
+        out_ref[y : y + 1, width:] = jnp.sum(
+            side[y * levels : (y + 1) * levels], axis=0, keepdims=True
+        )
 
 
 def diffuse(ring_a, ring_b, kappa_ref, edge_ref, rows, width, depth, adjoint):
@@ -124,16 +256,19 @@
     at_bottom = edge_ref[1] == 1
     source, target = ring_a, ring_b
     for step in range(1, depth + 1):
-        wanted = list(range(rows + depth - step)) + list(range(rows + depth + step, total))
+        wanted = list(range(rows + depth + step, total)) + list(range(rows + depth - step))
         keep = width if step == depth else 2 * width
+        plain, loaded = {}, {}
 
         def load(y):
-            value = source[y]
-            return kappa_ref[pl.ds(y, 1), :] * value if adjoint else value
+            if y not in loaded:
+                plain[y] = source[y]
+                loaded[y] = kappa_ref[pl.ds(y, 1), :] * plain[y] if adjoint else plain[y]
+            return loaded[y]
 
         for y in wanted:
+            north = load((y - 1) % total)
             center = load(y)
-            north = load((y - 1) % total)
             south = load((y + 1) % total)
             if y == 0:
                 north = jnp.where(at_top, center, north)
@@ -143,7 +278,7 @@
             east = pltpu.roll(center, 2 * width - 1, 1)
             change = ((north + south) + (west + east)) - 4.0 * center
             if adjoint:
-                result = source[y] + change
+                result = plain[y] + change
             else:
                 result = center + kappa_ref[pl.ds(y, 1), :] * change
             target[y, :, :keep] = result[:, :keep]
@@ -151,29 +286,32 @@
     return source
 
 
-def forward_kernel(
-    dims, ens_scale, edge_ref, alpha_ref, south_ref, north_ref, sides_ref, kappa_ref, vertical_ref,
-    perturb_ref, static_ref, out_ref, ring_a, ring_b, spread, acc,
-):
+def forward_kernel(dims, ens_scale, edge_ref, alpha_ref, kappa_ref, *refs):
     rows, levels, width, variables, depth = dims
+    halo, refs = refs[:8], refs[8:]
+    vertical_ref, perturb_ref, static_ref, out_ref, ring_ref, ring_a, ring_b, spread, acc = refs
     step = pl.program_id(0)
-    fill_ring(
-        lambda y: alpha_ref[0, pl.ds(y, levels, stride=rows), :],
-        south_ref, north_ref, sides_ref, ring_a, rows, levels, width, depth,
-    )
-    done = diffuse(ring_a, ring_b, kappa_ref, edge_ref, rows, width, depth, False)
-    for y in range(rows):
-        spread[pl.ds(y, levels, stride=rows), :] = jnp.dot(
-            vertical_ref[...], done[y, :, :width], precision=highest, preferred_element_type=f32
-        )
+    count = rows * levels
 
     @pl.when(step == 0)
     def _():
+        fill_kappa(kappa_ref, halo, ring_ref, rows, levels, width, depth)
         acc[...] = jnp.zeros_like(acc)
 
-    count = rows * levels
-    for v in range(variables):
-        acc[v * count : (v + 1) * count] += perturb_ref[0, v].astype(f32) * spread[...]
+    @pl.when(step > 0)
+    def _():
+        fill_ring(
+            lambda y: alpha_ref[0, pl.ds(y, levels, stride=rows), :],
+            halo, ring_a, rows, levels, width, depth,
+        )
+        done = diffuse(ring_a, ring_b, ring_ref, edge_ref, rows, width, depth, False)
+        for y in range(rows):
+            spread[pl.ds(y, levels, stride=rows), :] = jnp.dot(
+                vertical_ref[...], done[y, :, :width], precision=highest,
+                preferred_element_type=f32,
+            )
+        for v in range(variables):
+            acc[v * count : (v + 1) * count] += perturb_ref[0, v].astype(f32) * spread[...]
 
     @pl.when(step == pl.num_programs(0) - 1)
     def _():
@@ -204,15 +342,11 @@
     )
 
 
-def adjoint_kernel(
-    dims, edge_ref, alpha_ref, main_ref, south_ref, north_ref, sides_ref, kappa_ref, vertical_ref,
-    out_ref, ring_a, ring_b,
-):
+def adjoint_kernel(dims, edge_ref, alpha_ref, main_ref, *refs):
     rows, levels, width, variables, depth = dims
-    fill_ring(
-        lambda y: main_ref[0, y],
-        south_ref, north_ref, sides_ref, ring_a, rows, levels, width, depth,
-    )
+    halo, refs = refs[:8], refs[8:]
+    kappa_ref, vertical_ref, out_ref, ring_a, ring_b = refs
+    fill_ring(lambda y: main_ref[0, y], halo, ring_a, rows, levels, width, depth)
     done = diffuse(ring_a, ring_b, kappa_ref, edge_ref, rows, width, depth, True)
     for y in range(rows):
         out_ref[0, pl.ds(y, levels, stride=rows), :] = alpha_ref[
@@ -305,38 +439,55 @@
     smem = pl.BlockSpec(memory_space=pltpu.SMEM)
     vmem = pl.BlockSpec(memory_space=pltpu.VMEM)
     member_block = pl.BlockSpec((1, count, width), lambda k: (k, 0, 0))
-    row_block = pl.BlockSpec((1, depth, levels, width), lambda k: (k, 0, 0, 0))
-    side_block = pl.BlockSpec((1, 2 * depth, (rows + 2 * depth) * levels), lambda k: (k, 0, 0))
     perturb_block = pl.BlockSpec((1, variables, count, width), lambda k: (k, 0, 0, 0))
     ring_scratch = pltpu.VMEM((rows + 2 * depth, levels, 2 * width), f32)
-    edge_out, edge_specs = edge_shapes(members, rows, levels, width, depth)
 
     alpha_flat = alpha.reshape(members, count, width)
     perturb_flat = perturb.reshape(members, variables, count, width)
     vertical = vertical_matrix(vert_bounds, levels)
 
+    edge_out, edge_specs = edge_shapes(members + 1, rows, levels, width, depth)
     row_edges, col_edges = pl.pallas_call(
         lambda *refs: pack_kernel(rows, levels, depth, *refs),
-        grid=(members,),
-        in_specs=[member_block],
+        grid=(members + 1,),
+        in_specs=[
+            vmem,
+            pl.BlockSpec((1, count, width), lambda k: (jnp.minimum(k, members - 1), 0, 0)),
+        ],
         out_specs=edge_specs,
         out_shape=edge_out,
         compiler_params=params(1),
         name="pack",
-    )(alpha_flat)
-    south, north, sides = exchange(row_edges, col_edges, rows, levels, depth)
-    kappa_all = kappa_ring(kappa, depth)
+    )(kappa, alpha_flat)
+    halo = exchange(row_edges, col_edges, levels, depth, 0)
 
     static = jnp.einsum("vlm,vmyx->yxvl", static_vert, chi, precision=highest)
     static = jnp.where(me == 0, static_weight * static, 0.0).reshape(rows, width, column)
-    partial = pl.pallas_call(
+    partial, kappa_all = pl.pallas_call(
         lambda *refs: forward_kernel(dims, ens_scale, *refs),
-        grid=(members,),
+        grid=(members + 1,),
         in_specs=[
-            smem, member_block, row_block, row_block, side_block, vmem, vmem, perturb_block, vmem,
-        ],
-        out_specs=pl.BlockSpec((rows, width, column), lambda k: (0, 0, 0)),
-        out_shape=jax.ShapeDtypeStruct((rows, width, column), f32),
+            smem,
+            pl.BlockSpec((1, count, width), lambda k: (jnp.maximum(k - 1, 0), 0, 0)),
+            vmem,
+            *halo_specs(
+                members + 1, rows, levels, width, depth,
+                lambda k: jnp.where(k == 0, members, k - 1),
+            ),
+            vmem,
+            pl.BlockSpec(
+                (1, variables, count, width), lambda k: (jnp.maximum(k - 1, 0), 0, 0, 0)
+            ),
+            vmem,
+        ],
+        out_specs=[
+            pl.BlockSpec((rows, width, column), lambda k: (0, 0, 0)),
+            pl.BlockSpec((rows + 2 * depth, 2 * width), lambda k: (0, 0)),
+        ],
+        out_shape=[
+            jax.ShapeDtypeStruct((rows, width, column), f32),
+            jax.ShapeDtypeStruct((rows + 2 * depth, 2 * width), f32),
+        ],
         scratch_shapes=[
             ring_scratch,
             ring_scratch,
@@ -345,7 +496,7 @@
         ],
         compiler_params=params(1),
         name="forward",
-    )(edge, alpha_flat, south, north, sides, kappa_all, vertical, perturb_flat, static)
+    )(edge, alpha_flat, kappa, *halo, vertical, perturb_flat, static)
 
     east_rim = shifted(partial[:, :rim].astype(bf16), "gx", -1)
     wide = jnp.concatenate([partial, east_rim.astype(f32)], axis=1)
@@ -387,6 +538,7 @@
     west_rim = shifted(wide_grad[:, width:], "gx", 1)
     grad_cells = wide_grad[:, :width] + jnp.pad(west_rim, ((0, 0), (0, width - rim), (0, 0)))
 
+    edge_out, edge_specs = edge_shapes(members, rows, levels, width, depth)
     main, row_edges, col_edges = pl.pallas_call(
         lambda *refs: backward_kernel(dims, ens_scale, *refs),
         grid=(members,),
@@ -400,7 +552,7 @@
         compiler_params=params(1),
         name="backward",
     )(perturb_flat, grad_cells)
-    south, north, sides = exchange(row_edges, col_edges, rows, levels, depth)
+    halo = exchange(row_edges, col_edges, levels, depth, 1)
     grad_chi = chi + static_weight * jnp.einsum(
         "vlm,yxvl->vmyx",
         static_vert,
@@ -412,14 +564,14 @@
         grid=(members,),
         in_specs=[
             smem, member_block, pl.BlockSpec((1, rows, levels, width), lambda k: (k, 0, 0, 0)),
-            row_block, row_block, side_block, vmem, vmem,
+            *halo_specs(members, rows, levels, width, depth, lambda k: k), vmem, vmem,
         ],
         out_specs=member_block,
         out_shape=jax.ShapeDtypeStruct((members, count, width), f32),
         scratch_shapes=[ring_scratch, ring_scratch],
         compiler_params=params(1),
         name="adjoint",
-    )(edge, alpha_flat, main, south, north, sides, kappa_all, vertical.T)
+    )(edge, alpha_flat, main, *halo, kappa_all, vertical.T)
     return (grad_alpha.reshape(alpha.shape), grad_chi)
 
 

time: 151 us -> 138 us (0.914)
  starting transfers between devices: 35.9 us -> 3.42 us
  Pallas kernels: 57.9 us -> 87.7 us
  local copies, waits for them, and re-layouts: 14 us -> 7.9 us
  other arithmetic: 6.8 us -> 3.58 us
  waiting for transfers between devices: 28.4 us -> 26.3 us
    ppermute x10 -> x0, starting transfers between devices: 28 us -> none  [the longest x2 8.64 us: exchange(): corner_north = lax.ppermute(sides[:, :, -part:], 'gy', down)]
    pallas_call x0 -> x2, Pallas kernels: none -> 26 us  [exchange(): pl.pallas_call(lambda *refs: exchange_kernel(part, *refs), in_specs=[vmem...]
    squeeze x4 -> x0, local copies, waits for them, and re-layouts: 5.06 us -> none  [the longest x2 2.84 us: exchange(): north = lax.ppermute(row_edges[1], 'gy', down)]
    ppermute x10 -> x4, starting transfers between devices: 7.97 us -> 3.42 us  [shifted(): return lax.ppermute(value, axis, pairs)]
    pallas_call x1, Pallas kernels: 18.2 us -> 20.7 us  [body(): pl.pallas_call(lambda *refs: forward_kernel(dims, ens_scale, *refs), grid...]
    ppermute x10 -> x0, waiting for transfers between devices: 2.11 us -> none  [the longest x1 1.35 us: kappa_ring(): south = lax.ppermute(wide[:depth], 'gy', [(i, i - 1) for i in range(1, gy)])]
    concatenate x3 -> x0, other arithmetic: 2.02 us -> none  [the longest x2 1.35 us: exchange(): ring = jnp.concatenate([sides, corner_south, corner_north], axis=2)]
    unnamed x25 -> x13, local copies, waits for them, and re-layouts: 3.19 us -> 2.29 us
  transfers between devices with their start and end apart: 20 -> 4, of which waited for: 6 -> 4; matrix products, arithmetic and copies ran while one was open for 9% -> 0% of each run, Pallas kernels for 4% -> 0%
where the time goes in v2:
time: 138 us; the launch traced here: 137 us
  Pallas kernels  87.7 us (64%)
  waiting for transfers between devices  26.3 us (19%)
  local copies, waits for them, and re-layouts  7.9 us (6%)
  between operations  4.01 us (3%)
  matrix products  3.93 us (3%)
  other arithmetic  3.58 us (3%)
  starting transfers between devices  3.42 us (2%)
    ppermute x4, waiting for transfers between devices, shifted(): return lax.ppermute(value, axis, pairs)  26.3 us
    pallas_call x2, Pallas kernels, exchange(): pl.pallas_call(lambda *refs: exchange_kernel(part, *refs), in_specs=[vmem...  26 us
    pallas_call x1, Pallas kernels, body(): pl.pallas_call(lambda *refs: forward_kernel(dims, ens_scale, *refs), grid...  20.7 us
    pallas_call x1, Pallas kernels, body(): pl.pallas_call(lambda *refs: adjoint_kernel(dims, *refs), grid=(members,)...  17.4 us
    pallas_call x1, Pallas kernels, body(): pl.pallas_call(lambda *refs: observe_kernel(rows, band, padded, *refs), i...  9.44 us
    pallas_call x1, Pallas kernels, body(): pl.pallas_call(lambda *refs: backward_kernel(dims, ens_scale, *refs), gri...  7.93 us
    pallas_call x1, Pallas kernels, body(): pl.pallas_call(lambda *refs: pack_kernel(rows, levels, depth, *refs), gri...  6.2 us
    ppermute x4, starting transfers between devices, shifted(): return lax.ppermute(value, axis, pairs)  3.42 us
  transfers between devices with their start and end apart: 4, of which 4 were waited for; matrix products, arithmetic and copies ran while one was open for 0% of the time, Pallas kernels for 0%

profile of v2, /device:TPU:0, one launch (start us, length us, event | category | flops | bytes accessed | tf_op | source)
XLA Modules:
  0.0 136.9 jit_solution(4803582515348734563)
XLA Ops:
  0.7 0.8 slice_bitcast_fusion.1
  1.5 2.6 %fusion.3 = f32[16,128,4,32]{1,3,0,2:T(8,128)S(1)} fusion(f32[4,32,16,128]{3,2,1,0:T(8,128)} %param.16, pred[]{:T(512)S(6)} %eq.61, f32[4,32,32]{2,1,0:T(8,128)S(1)} %copy-done), kind=kOutput, calls=%fused_computation.7 | convolution fusion | flops 101187584 | bytes 2113537 | tf_op jit(solution)/shard_map/vlm,vmyx->yxvl/dot_general | solution.py:464
  4.2 1.3 copy.32.refs_13_
  5.5 0.6 add_convert_fusion.1.refs_0_
  6.1 0.7 exponential_select_fusion
  6.7 6.2 %pack.1 = (bf16[2,9,4,32,128]{4,3,2,1,0:T(8,128)(2,1)}, bf16[2,9,4,512]{3,2,1,0:T(4,128)(2,1)}) custom-call(f32[16,128]{1,0:T(8,128)} %refs_2_.1, f32[8,512,128]{2,1,0:T(8,128)} %bitcast.40), custom_call_target="tpu_custom_call" | custom-call | tf_op jit(solution)/shard_map/pack/pallas_call | solution.py:450
  12.9 14.3 %exchange.2 = (bf16[9,4,32,128]{3,2,1,0:T(8,128)(2,1)}, bf16[9,4,32,128]{3,2,1,0:T(8,128)(2,1)}, bf16[9,4,512]{2,1,0:T(4,128)(2,1)}, bf16[9,4,512]{2,1,0:T(4,128...) custom-call(bf16[2,9,4,32,128]{4,3,2,1,0:T(8,128)(2,1)} %get-tuple-e, ...), custom_call_target="tpu_custom_call" | custom-call | tf_op jit(solution)/shard_map/exchange/pallas_call | solution.py:199
  27.3 20.7 %forward.1 = (f32[16,128,128]{2,1,0:T(8,128)}, f32[24,256]{1,0:T(8,128)}) custom-call(s32[2]{0:T(128)} %add_convert_fusion.1.refs_0_, f32[8,512,128]{2,1,0:T(8,128)} %bitcast.41, f32[16,128]{1,0:T(8,128)} %refs_2_.1, bf16[9,4,32,128]{3,2,1,0:T(8,128)(2,1)} %get-tuple-element.27.refs_3_, bf16[9,4,32,128]{3,2,1,0:T(8,128)(2,1)} %get-tuple-element.28.refs_4_, ...), custom_call_target="tpu_custom_call" | custom-call | tf_op jit(solution)/shard_map/forward/pallas_call | solution.py:466
  48.0 1.1 slice.52
  49.2 0.7 fusion.12
  50.5 1.5 %collective-permute-done = bf16[16,33,128]{2,1,0:T(8,128)(2,1)S(1)} collective-permute-done((bf16[16,33,128]{2,1,0:T(8,128)(2,1)S(1)}, bf16[16,33,128]{2,1,0:T(8,128)(2,1)S(1)}, u32[]{:S(2)}, u32[]{:S(2)}) %collective-permute-start) | collective-permute-done | bytes 135200 | tf_op jit(solution)/shard_map/ppermute | solution.py:25
  52.0 1.2 select_convert_fusion
  53.2 1.6 %collective-permute-start.1 = (bf16[16,65,128]{2,1,0:T(8,128)(2,1)S(1)}, bf16[16,65,128]{2,1,0:T(8,128)(2,1)S(1)}, u32[]{:S(2)}, u32[]{:S(2)}) collective-permute-start(bf16[16,65,128]{2,1,0:T(8,128)(2,1)S(1)} %select_convert_fusion), channel_id=1, source_target_pairs={{0,16},{16,0},{1,17},{17,1},{2,18},{18,2},{3,19},{19,3},{4,20},{20... | collective-permute-start | bytes 798728 | tf_op jit(solution)/shard_map/ppermute | solution.py:25
  56.1 6.7 %collective-permute-done.1 = bf16[16,65,128]{2,1,0:T(8,128)(2,1)S(1)} collective-permute-done((bf16[16,65,128]{2,1,0:T(8,128)(2,1)S(1)}, bf16[16,65,128]{2,1,0:T(8,128)(2,1)S(1)}, u32[]{:S(2)}, u32[]{:S(2)}) %collective-permute-start.1) | collective-permute-done | bytes 266272 | tf_op jit(solution)/shard_map/ppermute | solution.py:25
  62.8 0.1 add_convert_fusion
  62.9 0.8 pad.16.refs_1_
  63.6 9.4 %observe.1 = f32[16,80,128]{2,1,0:T(8,128)} custom-call(s32[1]{0:T(128)S(6)} %copy.52.refs_0_, bf16[16,80,128]{2,1,0:T(8,128)(2,1)} %pad.16.refs_1_, s32[1,1024]{1,0:T(1,128)} %bitcast.48, f32[4,1024]{1,0:T(4,128)} %refs_3_.1, bf16[1024,128]{1,0:T(8,128)(2,1)} %refs_4_.1, f32[8,1024]{1,0:T(8,128)} %refs_5_.1, f32[8,1024]{1,0:T(8,128)} %refs_6_.1, ...), custom_call_target="tpu_custom_call" | custom-call | tf_op jit(solution)/shard_map/observe/pallas_call | solution.py:512
  73.1 1.2 slice.34
  74.2 0.1 copy.33
  74.4 1.6 %collective-permute-start.2 = (f32[16,65,128]{2,0,1:T(8,128)S(1)}, f32[16,65,128]{2,0,1:T(8,128)S(1)}, u32[]{:S(2)}, u32[]{:S(2)}) collective-permute-start(f32[16,65,128]{2,0,1:T(8,128)S(1)} %copy.33), channel_id=1, source_target_pairs={{0,16},{16,0},{1,17},{17,1},{2,18},{18,2},{3,19},{19,3},{4,20},{20... | collective-permute-start | bytes 1597448 | tf_op jit(solution)/shard_map/ppermute | solution.py:25
  77.0 11.6 %collective-permute-done.2 = f32[16,65,128]{2,0,1:T(8,128)S(1)} collective-permute-done((f32[16,65,128]{2,0,1:T(8,128)S(1)}, f32[16,65,128]{2,0,1:T(8,128)S(1)}, u32[]{:S(2)}, u32[]{:S(2)}) %collective-permute-start.2) | collective-permute-done | bytes 532512 | tf_op jit(solution)/shard_map/ppermute | solution.py:25
  88.7 0.2 copy_select_fusion
  88.9 0.2 collective-permute-start.3
  89.1 6.5 %collective-permute-done.3 = f32[16,33,128]{2,1,0:T(8,128)S(1)} collective-permute-done((f32[16,33,128]{2,1,0:T(8,128)S(1)}, f32[16,33,128]{2,1,0:T(8,128)S(1)}, u32[]{:S(2)}, u32[]{:S(2)}) %collective-permute-start.3) | collective-permute-done | bytes 270368 | tf_op jit(solution)/shard_map/ppermute | solution.py:25
  95.6 0.1 fusion.5.refs_1_
  95.7 0.3 copy.36
  96.1 0.6 copy-done.1
  96.7 7.9 %backward.1 = (f32[8,16,32,128]{3,2,1,0:T(8,128)}, bf16[2,8,4,32,128]{4,3,2,1,0:T(8,128)(2,1)}, bf16[2,8,4,512]{3,2,1,0:T(4,128)(2,1)}) custom-call(bf16[8,4,512,128]{3,2,1,0:T(8,128)(2,1)} %bitcast.44, f32[16,128,128]{2,1,0:T(8,128)} %copy-done.1), custom_call_target="tpu_custom_call" | custom-call | tf_op jit(solution)/shard_map/backward/pallas_call | solution.py:542
  104.6 1.3 fusion.1
  106.0 1.6 %copy.40 = f32[4,32,16,128]{3,2,1,0:T(8,128)} copy(f32[4,32,16,128]{3,1,2,0:T(8,128)S(1)} %fusion.1) | data formatting | bytes 2097152
  107.5 11.7 %exchange.3 = (bf16[8,4,32,128]{3,2,1,0:T(8,128)(2,1)}, bf16[8,4,32,128]{3,2,1,0:T(8,128)(2,1)}, bf16[8,4,512]{2,1,0:T(4,128)(2,1)}, bf16[8,4,512]{2,1,0:T(4,128...) custom-call(bf16[2,8,4,32,128]{4,3,2,1,0:T(8,128)(2,1)} %get-tuple-e, ...), custom_call_target="tpu_custom_call" | custom-call | tf_op jit(solution)/shard_map/exchange/pallas_call | solution.py:199
  119.3 17.4 %adjoint.1 = f32[8,512,128]{2,1,0:T(8,128)} custom-call(s32[2]{0:T(128)} %add_convert_fusion.1.refs_0_, f32[8,512,128]{2,1,0:T(8,128)} %bitcast.42, f32[8,16,32,128]{3,2,1,0:T(8,128)} %get-tuple-element.36.refs_2_, bf16[8,4,32,128]{3,2,1,0:T(8,128)(2,1)} %get-tuple-element.39.refs_3_, bf16[8,4,32,128]{3,2,1,0:T(8,128)(2,1)} %get-tuple-element.40.refs_4_, ...), custom_call_target="tpu_custom_call" | custom-call | tf_op jit(solution)/shard_map/adjoint/pallas_call | solution.py:562
  (15 shorter events, 0.3 us)
Async XLA Ops:
  0.6 0.8 copy-start
  27.3 21.9 %copy-start.5 = (s32[1,2]{1,0:T(1,128)S(1)}, s32[1,2]{1,0:T(1,128)}, u32[]{:S(2)}) copy-start(s32[1,2]{1,0:T(1,128)} %param.20) | copy-start | bytes 28
  48.0 14.8 %copy-start.2 = (f32[16,128,128]{2,1,0:T(8,128)S(1)}, f32[16,128,128]{2,1,0:T(8,128)}, u32[]{:S(2)}) copy-start(f32[16,128,128]{2,1,0:T(8,128)} %get-tuple-element.35) | copy-start | bytes 3145732
  49.1 2.9 %collective-permute-start = (bf16[16,33,128]{2,1,0:T(8,128)(2,1)S(1)}, bf16[16,33,128]{2,1,0:T(8,128)(2,1)S(1)}, u32[]{:S(2)}, u32[]{:S(2)}) collective-permute-start(bf16[16,33,128]{2,1,0:T(8,128)(2,1)S(1)} %slice.52), channel_id=1, source_target_pairs={{0,3},{1,0},{2,1},{3,2},{4,7},{5,4},{6,5},{7,6},{8,11},{9,8},{10,9... | collective-permute-start | bytes 405512 | tf_op jit(solution)/shard_map/ppermute | solution.py:25
  53.2 9.5 %collective-permute-start.1 = (bf16[16,65,128]{2,1,0:T(8,128)(2,1)S(1)}, bf16[16,65,128]{2,1,0:T(8,128)(2,1)S(1)}, u32[]{:S(2)}, u32[]{:S(2)}) collective-permute-start(bf16[16,65,128]{2,1,0:T(8,128)(2,1)S(1)} %select_convert_fusion), channel_id=1, source_target_pairs={{0,16},{16,0},{1,17},{17,1},{2,18},{18,2},{3,19},{19,3},{4,20},{20... | collective-permute-start | bytes 798728 | tf_op jit(solution)/shard_map/ppermute | solution.py:25
  73.1 15.6 %copy-start.3 = (f32[16,80,128]{2,1,0:T(8,128)S(1)}, f32[16,80,128]{2,1,0:T(8,128)}, u32[]{:S(2)}) copy-start(f32[16,80,128]{2,1,0:T(8,128)} %observe.1) | copy-start | bytes 1966084
  74.4 14.3 %collective-permute-start.2 = (f32[16,65,128]{2,0,1:T(8,128)S(1)}, f32[16,65,128]{2,0,1:T(8,128)S(1)}, u32[]{:S(2)}, u32[]{:S(2)}) collective-permute-start(f32[16,65,128]{2,0,1:T(8,128)S(1)} %copy.33), channel_id=1, source_target_pairs={{0,16},{16,0},{1,17},{17,1},{2,18},{18,2},{3,19},{19,3},{4,20},{20... | collective-permute-start | bytes 1597448 | tf_op jit(solution)/shard_map/ppermute | solution.py:25
  88.9 6.7 %collective-permute-start.3 = (f32[16,33,128]{2,1,0:T(8,128)S(1)}, f32[16,33,128]{2,1,0:T(8,128)S(1)}, u32[]{:S(2)}, u32[]{:S(2)}) collective-permute-start(f32[16,33,128]{2,1,0:T(8,128)S(1)} %pad_add_fusion), channel_id=1, source_target_pairs={{0,1},{1,2},{2,3},{3,0},{4,5},{5,6},{6,7},{7,4},{8,9},{9,10},{10,1... | collective-permute-start | bytes 811016 | tf_op jit(solution)/shard_map/ppermute | solution.py:25
  95.7 1.0 copy-start.1
  96.7 7.9 %copy-start.4 = (f32[4,32,16,128]{3,2,1,0:T(8,128)S(1)}, f32[4,32,16,128]{3,2,1,0:T(8,128)}, u32[]{:S(2)}) copy-start(f32[4,32,16,128]{3,2,1,0:T(8,128)} %param.16) | copy-start | bytes 3145732

commit v3 on v2

--- a/solution.py
+++ b/solution.py
@@ -207,53 +207,46 @@
     )(row_edges, col_edges)
 
 
-def halo_specs(members, rows, levels, width, depth, place):
-    row = pl.BlockSpec((1, depth, levels, width), lambda k: (place(k), 0, 0, 0))
-    side = pl.BlockSpec((1, depth, rows * levels), lambda k: (place(k), 0, 0))
-    corner = pl.BlockSpec((1, depth, depth * levels), lambda k: (place(k), 0, 0))
-    return [row, row, side, side, corner, corner, corner, corner]
-
-
-def side_lanes(halo, width, depth):
+def side_lanes(halo, member, width, depth):
     south, north, east, west, south_east, south_west, north_east, north_west = halo
     picker = edge_picker(width, depth).astype(bf16)
-    easts = jnp.concatenate([east[0], south_east[0], north_east[0]], axis=1)
-    wests = jnp.concatenate([west[0], south_west[0], north_west[0]], axis=1)
+    easts = jnp.concatenate([east[member], south_east[member], north_east[member]], axis=1)
+    wests = jnp.concatenate([west[member], south_west[member], north_west[member]], axis=1)
     return lax.dot_general(
         easts, picker[:depth], TN, preferred_element_type=f32
     ) + lax.dot_general(wests, picker[depth:], TN, preferred_element_type=f32)
 
 
-def fill_ring(tile, halo, ring, rows, levels, width, depth):
+def fill_ring(tile, halo, member, ring, rows, levels, width, depth):
     total = rows + 2 * depth
     for y in range(rows):
         ring[y, :, :width] = tile(y)
     for d in range(depth):
-        ring[rows + d, :, :width] = halo[0][0, d].astype(f32)
-        ring[rows + depth + d, :, :width] = halo[1][0, d].astype(f32)
-    side = side_lanes(halo, width, depth)
+        ring[rows + d, :, :width] = halo[0][member, d].astype(f32)
+        ring[rows + depth + d, :, :width] = halo[1][member, d].astype(f32)
+    side = side_lanes(halo, member, width, depth)
     for y in range(total):
         ring[y, :, width:] = side[y * levels : (y + 1) * levels]
 
 
-def fill_kappa(kappa_ref, halo, out_ref, rows, levels, width, depth):
+def fill_kappa(kappa_ref, halo, member, out_ref, rows, levels, width, depth):
     out_ref[:rows, :width] = kappa_ref[...]
     for d in range(depth):
         for base, ref in ((rows, halo[0]), (rows + depth, halo[1])):
             out_ref[base + d : base + d + 1, :width] = jnp.sum(
-                ref[0, d].astype(f32), axis=0, keepdims=True
+                ref[member, d].astype(f32), axis=0, keepdims=True
             )
-    side = side_lanes(halo, width, depth)
+    side = side_lanes(halo, member, width, depth)
     for y in range(rows + 2 * depth):
         out_ref[y : y + 1, width:] = jnp.sum(
             side[y * levels : (y + 1) * levels], axis=0, keepdims=True
         )
 
 
-def diffuse(ring_a, ring_b, kappa_ref, edge_ref, rows, width, depth, adjoint):
+def diffuse(ring_a, ring_b, kappa_ref, rows, width, depth, adjoint):
     total = rows + 2 * depth
-    at_top = edge_ref[0] == 1
-    at_bottom = edge_ref[1] == 1
+    at_top = lax.axis_index("gy") == 0
+    at_bottom = lax.axis_index("gy") == lax.axis_size("gy") - 1
     source, target = ring_a, ring_b
     for step in range(1, depth + 1):
         wanted = list(range(rows + depth + step, total)) + list(range(rows + depth - step))
@@ -286,7 +279,7 @@
     return source
 
 
-def forward_kernel(dims, ens_scale, edge_ref, alpha_ref, kappa_ref, *refs):
+def forward_kernel(dims, ens_scale, alpha_ref, kappa_ref, *refs):
     rows, levels, width, variables, depth = dims
     halo, refs = refs[:8], refs[8:]
     vertical_ref, perturb_ref, static_ref, out_ref, ring_ref, ring_a, ring_b, spread, acc = refs
@@ -295,16 +288,16 @@
 
     @pl.when(step == 0)
     def _():
-        fill_kappa(kappa_ref, halo, ring_ref, rows, levels, width, depth)
+        fill_kappa(kappa_ref, halo, halo[0].shape[0] - 1, ring_ref, rows, levels, width, depth)
         acc[...] = jnp.zeros_like(acc)
 
     @pl.when(step > 0)
     def _():
         fill_ring(
             lambda y: alpha_ref[0, pl.ds(y, levels, stride=rows), :],
-            halo, ring_a, rows, levels, width, depth,
-        )
-        done = diffuse(ring_a, ring_b, ring_ref, edge_ref, rows, width, depth, False)
+            halo, step - 1, ring_a, rows, levels, width, depth,
+        )
+        done = diffuse(ring_a, ring_b, ring_ref, rows, width, depth, False)
         for y in range(rows):
             spread[pl.ds(y, levels, stride=rows), :] = jnp.dot(
                 vertical_ref[...], done[y, :, :width], precision=highest,
@@ -342,12 +335,12 @@
     )
 
 
-def adjoint_kernel(dims, edge_ref, alpha_ref, main_ref, *refs):
+def adjoint_kernel(dims, alpha_ref, main_ref, *refs):
     rows, levels, width, variables, depth = dims
     halo, refs = refs[:8], refs[8:]
     kappa_ref, vertical_ref, out_ref, ring_a, ring_b = refs
-    fill_ring(lambda y: main_ref[0, y], halo, ring_a, rows, levels, width, depth)
-    done = diffuse(ring_a, ring_b, kappa_ref, edge_ref, rows, width, depth, True)
+    fill_ring(lambda y: main_ref[0, y], halo, pl.program_id(0), ring_a, rows, levels, width, depth)
+    done = diffuse(ring_a, ring_b, kappa_ref, rows, width, depth, True)
     for y in range(rows):
         out_ref[0, pl.ds(y, levels, stride=rows), :] = alpha_ref[
             0, pl.ds(y, levels, stride=rows), :
@@ -428,8 +421,6 @@
     places = obs_stencil.shape[0]
     dims = (rows, levels, width, variables, depth)
     ens_scale = ensemble_weight / math.sqrt(members * groups - 1)
-    gy_place = lax.axis_index("gy")
-    edge = jnp.stack([gy_place == 0, gy_place == lax.axis_size("gy") - 1]).astype(jnp.int32)
     owners = fine_owner[0]
     band_ids = lax.iota(jnp.int32, groups)
 
@@ -467,13 +458,9 @@
         lambda *refs: forward_kernel(dims, ens_scale, *refs),
         grid=(members + 1,),
         in_specs=[
-            smem,
             pl.BlockSpec((1, count, width), lambda k: (jnp.maximum(k - 1, 0), 0, 0)),
             vmem,
-            *halo_specs(
-                members + 1, rows, levels, width, depth,
-                lambda k: jnp.where(k == 0, members, k - 1),
-            ),
+            *[vmem] * 8,
             vmem,
             pl.BlockSpec(
                 (1, variables, count, width), lambda k: (jnp.maximum(k - 1, 0), 0, 0, 0)
@@ -496,16 +483,21 @@
         ],
         compiler_params=params(1),
         name="forward",
-    )(edge, alpha_flat, kappa, *halo, vertical, perturb_flat, static)
-
+    )(alpha_flat, kappa, *halo, vertical, perturb_flat, static)
+
+    own_band = band_of(me)
     east_rim = shifted(partial[:, :rim].astype(bf16), "gx", -1)
-    wide = jnp.concatenate([partial, east_rim.astype(f32)], axis=1)
-    regions = [wide[:, b * band + shift : b * band + shift + band + 1] for b in range(groups)]
-    own_band = band_of(me)
-    increment = choose(own_band, regions)
-    for hop in range(1, groups):
-        away = choose(band_of((me + hop) % groups), regions).astype(bf16)
-        increment = increment + shifted(away, "mem", hop).astype(f32)
+    near = [partial[:, b * band + shift : (b + 1) * band] for b in range(groups)]
+    far = [partial[:, b * band : b * band + rim] for b in range(1, groups)]
+    far.append(east_rim.astype(f32))
+    halves = []
+    for parts in (near, far):
+        half = choose(own_band, parts)
+        for hop in range(1, groups):
+            away = choose(band_of((me + hop) % groups), parts).astype(bf16)
+            half = half + shifted(away, "mem", hop).astype(f32)
+        halves.append(half)
+    increment = jnp.concatenate(halves, axis=1)
     padded = -(-(band + 1) // 16) * 16
     table = jnp.pad(increment.astype(bf16), ((0, 0), (0, padded - band - 1), (0, 0)))
 
@@ -525,18 +517,27 @@
         inv_var, jacobian,
     )
 
-    region_grad = region_grad[:, : band + 1]
-    pieces = [(own_band, region_grad)]
+    near, far = region_grad[:, : band - shift], region_grad[:, band - shift : band + 1]
+    far_pieces = [(own_band, far)]
     for hop in range(1, groups):
-        pieces.append((band_of((me - hop) % groups), shifted(region_grad, "mem", hop)))
-    wide_grad = jnp.zeros((rows, width + rim, column), f32)
+        far_pieces.append((band_of((me - hop) % groups), shifted(far, "mem", hop)))
+    rim_grad = choose_equal(groups - 1, far_pieces)
+    near, rim_grad = lax.optimization_barrier((near, rim_grad))
+    west_rim = shifted(rim_grad, "gx", 1)
+    near_pieces = [(own_band, near)]
+    for hop in range(1, groups):
+        near_pieces.append((band_of((me - hop) % groups), shifted(near, "mem", hop)))
+    grad_cells = jnp.pad(west_rim, ((0, 0), (0, width - rim), (0, 0)))
     for b in range(groups):
-        placed = choose_equal(b, pieces)
         before = b * band + shift
-        after = width + rim - before - band - 1
-        wide_grad = wide_grad + jnp.pad(placed, ((0, 0), (before, after), (0, 0)))
-    west_rim = shifted(wide_grad[:, width:], "gx", 1)
-    grad_cells = wide_grad[:, :width] + jnp.pad(west_rim, ((0, 0), (0, width - rim), (0, 0)))
+        grad_cells = grad_cells + jnp.pad(
+            choose_equal(b, near_pieces), ((0, 0), (before, width - (b + 1) * band), (0, 0))
+        )
+    for b in range(1, groups):
+        before = b * band
+        grad_cells = grad_cells + jnp.pad(
+            choose_equal(b - 1, far_pieces), ((0, 0), (before, width - before - rim), (0, 0))
+        )
 
     edge_out, edge_specs = edge_shapes(members, rows, levels, width, depth)
     main, row_edges, col_edges = pl.pallas_call(
@@ -563,15 +564,15 @@
         lambda *refs: adjoint_kernel(dims, *refs),
         grid=(members,),
         in_specs=[
-            smem, member_block, pl.BlockSpec((1, rows, levels, width), lambda k: (k, 0, 0, 0)),
-            *halo_specs(members, rows, levels, width, depth, lambda k: k), vmem, vmem,
+            member_block, pl.BlockSpec((1, rows, levels, width), lambda k: (k, 0, 0, 0)),
+            *[vmem] * 8, vmem, vmem,
         ],
         out_specs=member_block,
         out_shape=jax.ShapeDtypeStruct((members, count, width), f32),
         scratch_shapes=[ring_scratch, ring_scratch],
         compiler_params=params(1),
         name="adjoint",
-    )(edge, alpha_flat, main, *halo, kappa_all, vertical.T)
+    )(alpha_flat, main, *halo, kappa_all, vertical.T)
     return (grad_alpha.reshape(alpha.shape), grad_chi)
 
 

time: 138 us -> 133 us (0.964)
  waiting for transfers between devices: 26.3 us -> 17.1 us
  other arithmetic: 3.58 us -> 7.49 us
    ppermute x4 -> x6, waiting for transfers between devices: 26.3 us -> 17.1 us  [shifted(): return lax.ppermute(value, axis, pairs)]
    another operation x0 -> x2, other arithmetic: none -> 2.13 us
    ppermute x4 -> x6, starting transfers between devices: 3.42 us -> 3.88 us  [shifted(): return lax.ppermute(value, axis, pairs)]
  transfers between devices with their start and end apart: 4 -> 6, of which waited for: 4 -> 5; matrix products, arithmetic and copies ran while one was open for 0% -> 4% of each run, Pallas kernels for 0% -> 0%
where the time goes in v3:
time: 133 us; the launch traced here: 132 us
  Pallas kernels  87.5 us (66%)
  waiting for transfers between devices  17.1 us (13%)
  local copies, waits for them, and re-layouts  7.74 us (6%)
  other arithmetic  7.49 us (6%)
  between operations  4 us (3%)
  matrix products  3.93 us (3%)
  starting transfers between devices  3.88 us (3%)
    pallas_call x2, Pallas kernels, exchange(): pl.pallas_call(lambda *refs: exchange_kernel(part, *refs), in_specs=[vmem...  25.8 us
    pallas_call x1, Pallas kernels, body(): pl.pallas_call(lambda *refs: forward_kernel(dims, ens_scale, *refs), grid...  20.6 us
    pallas_call x1, Pallas kernels, body(): pl.pallas_call(lambda *refs: adjoint_kernel(dims, *refs), grid=(members,)...  17.5 us
    ppermute x6, waiting for transfers between devices, shifted(): return lax.ppermute(value, axis, pairs)  17.1 us
    pallas_call x1, Pallas kernels, body(): pl.pallas_call(lambda *refs: observe_kernel(rows, band, padded, *refs), i...  9.45 us
    pallas_call x1, Pallas kernels, body(): pl.pallas_call(lambda *refs: backward_kernel(dims, ens_scale, *refs), gri...  7.93 us
    pallas_call x1, Pallas kernels, body(): pl.pallas_call(lambda *refs: pack_kernel(rows, levels, depth, *refs), gri...  6.2 us
    ppermute x6, starting transfers between devices, shifted(): return lax.ppermute(value, axis, pairs)  3.88 us
  transfers between devices with their start and end apart: 6, of which 5 were waited for; matrix products, arithmetic and copies ran while one was open for 4% of the time, Pallas kernels for 0%

profile of v3, /device:TPU:0, one launch (start us, length us, event | category | flops | bytes accessed | tf_op | source)
XLA Modules:
  0.0 131.7 jit_solution(10413202426936195573)
XLA Ops:
  0.6 0.8 slice_bitcast_fusion.1
  1.5 2.6 %fusion.3 = f32[16,128,4,32]{1,3,0,2:T(8,128)S(1)} fusion(f32[4,32,16,128]{3,2,1,0:T(8,128)} %param.16, pred[]{:T(512)S(6)} %eq.59, f32[4,32,32]{2,1,0:T(8,128)S(1)} %copy-done), kind=kOutput, calls=%fused_computation.5 | convolution fusion | flops 101187584 | bytes 2113537 | tf_op jit(solution)/shard_map/vlm,vmyx->yxvl/dot_general | solution.py:455
  4.2 1.3 copy.24.refs_12_
  5.5 0.7 exponential_select_fusion
  6.2 6.2 %pack.1 = (bf16[2,9,4,32,128]{4,3,2,1,0:T(8,128)(2,1)}, bf16[2,9,4,512]{3,2,1,0:T(4,128)(2,1)}) custom-call(f32[16,128]{1,0:T(8,128)} %refs_1_.1, f32[8,512,128]{2,1,0:T(8,128)} %bitcast.38), custom_call_target="tpu_custom_call" | custom-call | tf_op jit(solution)/shard_map/pack/pallas_call | solution.py:441
  12.4 14.3 %exchange.2 = (bf16[9,4,32,128]{3,2,1,0:T(8,128)(2,1)}, bf16[9,4,32,128]{3,2,1,0:T(8,128)(2,1)}, bf16[9,4,512]{2,1,0:T(4,128)(2,1)}, bf16[9,4,512]{2,1,0:T(4,128...) custom-call(bf16[2,9,4,32,128]{4,3,2,1,0:T(8,128)(2,1)} %get-tuple-e, ...), custom_call_target="tpu_custom_call" | custom-call | tf_op jit(solution)/shard_map/exchange/pallas_call | solution.py:199
  26.7 20.6 %forward.1 = (f32[16,128,128]{2,1,0:T(8,128)}, f32[24,256]{1,0:T(8,128)}) custom-call(f32[8,512,128]{2,1,0:T(8,128)} %bitcast.39, f32[16,128]{1,0:T(8,128)} %refs_1_.1, bf16[9,4,32,128]{3,2,1,0:T(8,128)(2,1)} %get-tuple-element.29.refs_2_, bf16[9,4,32,128]{3,2,1,0:T(8,128)(2,1)} %get-tuple-element.30.refs_3_, bf16[9,4,512]{2,1,0:T(4,128)(2,1)} %get-tuple-element.31.refs_4_, ...), custom_call_target="tpu_custom_call" | custom-call | tf_op jit(solution)/shard_map/forward/pallas_call | solution.py:457
  47.3 1.0 slice.47
  48.4 0.7 fusion.18
  49.8 1.1 select_convert_fusion
  50.8 1.6 %collective-permute-start = (bf16[16,32,128]{2,1,0:T(8,128)(2,1)S(1)}, bf16[16,32,128]{2,1,0:T(8,128)(2,1)S(1)}, u32[]{:S(2)}, u32[]{:S(2)}) collective-permute-start(bf16[16,32,128]{2,1,0:T(8,128)(2,1)S(1)} %select_convert_fusion), channel_id=1, source_target_pairs={{0,16},{16,0},{1,17},{17,1},{2,18},{18,2},{3,19},{19,3},{4,20},{20... | collective-permute-start | bytes 393224 | tf_op jit(solution)/shard_map/ppermute | solution.py:25
  53.7 1.0 fusion.10
  55.3 1.4 %collective-permute-done = bf16[16,32,128]{2,1,0:T(8,128)(2,1)S(1)} collective-permute-done((bf16[16,32,128]{2,1,0:T(8,128)(2,1)S(1)}, bf16[16,32,128]{2,1,0:T(8,128)(2,1)S(1)}, u32[]{:S(2)}, u32[]{:S(2)}) %collective-permute-start) | collective-permute-done | bytes 131104 | tf_op jit(solution)/shard_map/ppermute | solution.py:25
  56.8 1.1 add_convert_fusion
  57.9 3.2 %collective-permute-done.2 = bf16[16,33,128]{2,1,0:T(8,128)(2,1)S(1)} collective-permute-done((bf16[16,33,128]{2,1,0:T(8,128)(2,1)S(1)}, bf16[16,33,128]{2,1,0:T(8,128)(2,1)S(1)}, u32[]{:S(2)}, u32[]{:S(2)}) %collective-permute-start.2) | collective-permute-done | bytes 135200 | tf_op jit(solution)/shard_map/ppermute | solution.py:25
  61.1 1.0 fusion.9
  62.1 0.8 fusion.11.refs_1_
  62.9 9.4 %observe.1 = f32[16,80,128]{2,1,0:T(8,128)} custom-call(s32[1]{0:T(128)S(6)} %copy.39.refs_0_, bf16[16,80,128]{2,1,0:T(8,128)(2,1)} %fusion.11.refs_1_, s32[1,1024]{1,0:T(1,128)} %bitcast.46, f32[4,1024]{1,0:T(4,128)} %refs_3_.1, bf16[1024,128]{1,0:T(8,128)(2,1)} %refs_4_.1, f32[8,1024]{1,0:T(8,128)} %refs_5_.1, f32[8,1024]{1,0:T(8,128)} %refs_6_.1, ...), custom_call_target="tpu_custom_call" | custom-call | tf_op jit(solution)/shard_map/observe/pallas_call | solution.py:504
  72.3 1.0 slice.35
  73.3 0.8 collective-permute-start.3
  75.3 1.0 slice.34
  76.3 6.0 %collective-permute-done.3 = f32[16,33,128]{2,1,0:T(8,128)S(1)} collective-permute-done((f32[16,33,128]{2,1,0:T(8,128)S(1)}, f32[16,33,128]{2,1,0:T(8,128)S(1)}, u32[]{:S(2)}, u32[]{:S(2)}) %collective-permute-start.3) | collective-permute-done | bytes 270368 | tf_op jit(solution)/shard_map/ppermute | solution.py:25
  82.3 1.0 broadcast_select_fusion.1
  83.4 0.9 collective-permute-start.5
  84.3 5.8 %collective-permute-done.5 = f32[16,32,128]{2,1,0:T(8,128)S(1)} collective-permute-done((f32[16,32,128]{2,1,0:T(8,128)S(1)}, f32[16,32,128]{2,1,0:T(8,128)S(1)}, u32[]{:S(2)}, u32[]{:S(2)}) %collective-permute-start.5) | collective-permute-done | bytes 262176 | tf_op jit(solution)/shard_map/ppermute | solution.py:25
  90.2 0.6 collective-permute-done.4
  91.2 0.6 copy-done.1
  91.9 7.9 %backward.1 = (f32[8,16,32,128]{3,2,1,0:T(8,128)}, bf16[2,8,4,32,128]{4,3,2,1,0:T(8,128)(2,1)}, bf16[2,8,4,512]{3,2,1,0:T(4,128)(2,1)}) custom-call(bf16[8,4,512,128]{3,2,1,0:T(8,128)(2,1)} %bitcast.42, f32[16,128,128]{2,1,0:T(8,128)} %copy-done.1), custom_call_target="tpu_custom_call" | custom-call | tf_op jit(solution)/shard_map/backward/pallas_call | solution.py:543
  99.8 1.3 %fusion.1 = f32[4,32,16,128]{3,1,2,0:T(8,128)S(1)} fusion(f32[16,128,4,32]{1,3,2,0:T(8,128)S(1)} %bitcast.43, f32[4,32,16,128]{3,2,1,0:T(8,128)S(1)} %copy-done.2, f32[4,32,32]{2,1,0:T(8,128)S(1)} %copy-done), kind=kOutput, calls=%fused_computation.2 | convolution fusion | flops 101187584 | bytes 3162112 | tf_op jit(solution)/shard_map/vlm,yxvl->vmyx/dot_general | solution.py:557
  101.1 1.6 %copy.29 = f32[4,32,16,128]{3,2,1,0:T(8,128)} copy(f32[4,32,16,128]{3,1,2,0:T(8,128)S(1)} %fusion.1) | data formatting | bytes 2097152
  102.7 11.5 %exchange.3 = (bf16[8,4,32,128]{3,2,1,0:T(8,128)(2,1)}, bf16[8,4,32,128]{3,2,1,0:T(8,128)(2,1)}, bf16[8,4,512]{2,1,0:T(4,128)(2,1)}, bf16[8,4,512]{2,1,0:T(4,128...) custom-call(bf16[2,8,4,32,128]{4,3,2,1,0:T(8,128)(2,1)} %get-tuple-e, ...), custom_call_target="tpu_custom_call" | custom-call | tf_op jit(solution)/shard_map/exchange/pallas_call | solution.py:199
  114.2 17.5 %adjoint.1 = f32[8,512,128]{2,1,0:T(8,128)} custom-call(f32[8,512,128]{2,1,0:T(8,128)} %bitcast.40, f32[8,16,32,128]{3,2,1,0:T(8,128)} %get-tuple-element.40.refs_1_, bf16[8,4,32,128]{3,2,1,0:T(8,128)(2,1)} %get-tuple-element.43.refs_2_, bf16[8,4,32,128]{3,2,1,0:T(8,128)(2,1)} %get-tuple-element.44.refs_3_, bf16[8,4,512]{2,1,0:T(4,128)(2,1)} %get-tuple-element.45.refs_4_, ...), custom_call_target="tpu_custom_call" | custom-call | tf_op jit(solution)/shard_map/adjoint/pallas_call | solution.py:563
  (15 shorter events, 1.3 us)
Async XLA Ops:
  0.6 0.8 copy-start
  26.7 21.7 %copy-start.3 = (s32[1,2]{1,0:T(1,128)S(1)}, s32[1,2]{1,0:T(1,128)}, u32[]{:S(2)}) copy-start(s32[1,2]{1,0:T(1,128)} %param.20) | copy-start | bytes 28
  48.3 5.4 %collective-permute-start.1 = (bf16[16,33,128]{2,1,0:T(8,128)(2,1)S(1)}, bf16[16,33,128]{2,1,0:T(8,128)(2,1)S(1)}, u32[]{:S(2)}, u32[]{:S(2)}) collective-permute-start(bf16[16,33,128]{2,1,0:T(8,128)(2,1)S(1)} %slice.47), channel_id=1, source_target_pairs={{0,3},{1,0},{2,1},{3,2},{4,7},{5,4},{6,5},{7,6},{8,11},{9,8},{10,9... | collective-permute-start | bytes 405512 | tf_op jit(solution)/shard_map/ppermute | solution.py:25
  50.8 5.9 %collective-permute-start = (bf16[16,32,128]{2,1,0:T(8,128)(2,1)S(1)}, bf16[16,32,128]{2,1,0:T(8,128)(2,1)S(1)}, u32[]{:S(2)}, u32[]{:S(2)}) collective-permute-start(bf16[16,32,128]{2,1,0:T(8,128)(2,1)S(1)} %select_convert_fusion), channel_id=1, source_target_pairs={{0,16},{16,0},{1,17},{17,1},{2,18},{18,2},{3,19},{19,3},{4,20},{20... | collective-permute-start | bytes 393224 | tf_op jit(solution)/shard_map/ppermute | solution.py:25
  54.7 6.4 %collective-permute-start.2 = (bf16[16,33,128]{2,1,0:T(8,128)(2,1)S(1)}, bf16[16,33,128]{2,1,0:T(8,128)(2,1)S(1)}, u32[]{:S(2)}, u32[]{:S(2)}) collective-permute-start(bf16[16,33,128]{2,1,0:T(8,128)(2,1)S(1)} %fusion.10), channel_id=1, source_target_pairs={{0,16},{16,0},{1,17},{17,1},{2,18},{18,2},{3,19},{19,3},{4,20},{20... | collective-permute-start | bytes 405512 | tf_op jit(solution)/shard_map/ppermute | solution.py:25
  73.3 9.0 %collective-permute-start.3 = (f32[16,33,128]{2,1,0:T(8,128)S(1)}, f32[16,33,128]{2,1,0:T(8,128)S(1)}, u32[]{:S(2)}, u32[]{:S(2)}) collective-permute-start(f32[16,33,128]{2,1,0:T(8,128)S(1)} %slice.35), channel_id=1, source_target_pairs={{0,16},{16,0},{1,17},{17,1},{2,18},{18,2},{3,19},{19,3},{4,20},{20... | collective-permute-start | bytes 811016 | tf_op jit(solution)/shard_map/ppermute | solution.py:25
  83.4 6.8 %collective-permute-start.5 = (f32[16,32,128]{2,1,0:T(8,128)S(1)}, f32[16,32,128]{2,1,0:T(8,128)S(1)}, u32[]{:S(2)}, u32[]{:S(2)}) collective-permute-start(f32[16,32,128]{2,1,0:T(8,128)S(1)} %slice.34), channel_id=1, source_target_pairs={{0,16},{16,0},{1,17},{17,1},{2,18},{18,2},{3,19},{19,3},{4,20},{20... | collective-permute-start | bytes 786440 | tf_op jit(solution)/shard_map/ppermute | solution.py:25
  84.3 6.5 %collective-permute-start.4 = (f32[16,33,128]{2,1,0:T(8,128)S(1)}, f32[16,33,128]{2,1,0:T(8,128)S(1)}, u32[]{:S(2)}, u32[]{:S(2)}) collective-permute-start(f32[16,33,128]{2,1,0:T(8,128)S(1)} %get-tuple-element.38), channel_id=1, source_target_pairs={{0,1},{1,2},{2,3},{3,0},{4,5},{5,6},{6,7},{7,4},{8,9},{9,10},{10,1... | collective-permute-start | bytes 811016 | tf_op jit(solution)/shard_map/ppermute | solution.py:25
  90.9 1.0 copy-start.1
  91.9 7.9 %copy-start.2 = (f32[4,32,16,128]{3,2,1,0:T(8,128)S(1)}, f32[4,32,16,128]{3,2,1,0:T(8,128)}, u32[]{:S(2)}) copy-start(f32[4,32,16,128]{3,2,1,0:T(8,128)} %param.16) | copy-start | bytes 3145732
